TPU v7x, 512 devices: a whole 4x8x8 slice. The times are simulated.
512 devices in a mesh: tm: 32 (over z, x), frac: 16 (over y, core).
Axes of the slice: x: 4, y: 8, z: 8, core: 2. Of those that a mesh axis runs over, the one named last changes fastest.
Arguments:
- pressure0: float32 [64, 32, 128], P('frac'), may hold values from -6 to 6
- storage: float32 [64, 32, 128], P('frac'), may hold values from 0.1 to 1
- perm_base: float32 [64, 32, 128], P('frac'), may hold values from 0.2 to 5
- leakoff: float32 [64, 32, 128], P('frac'), may hold values from 0.5 to 2
- sources: float32 [32, 64, 32, 128], P('tm', 'frac'), may hold values from -6 to 6
- export_cells: int32 [4096], P('frac'), may hold values from 0 to 16383
- inter_local: int32 [16384], P('frac'), may hold values from 0 to 16383
- trace_source: int32 [16384], P('frac'), may hold values from 0 to 4095, as said below
- inter_trans: float32 [16384], P('frac'), may hold values from 0.5 to 4
- inter_count: int32 [16], P('frac'), may hold values from 1 to 1024, 8192 in all
Outputs:
- slice_pressure: float32 [32, 64, 32, 128], P('tm', 'frac')
Inputs may be any that keep to these rules, and one draw needn't show every extreme that they name: An entry of frac index d names a slot of another frac index: trace_source // 256 differs from d. `inter_count`: the live entries of a frac index are its first ones; the largest count is 1024.
All inputs are finite; a program needn't handle non-finite values. No bound on the sum of `inter_count` on one device may be relied on, other than what follows from the above.
Results may differ from a plain program's by a relative error of at most 0.00002.
Values sent between devices are 32-bit elements; how exact they have to be, the bound alone decides.
A program may use at most 64 MiB of HBM per device.

v0:
```python
import jax
import jax.numpy as jnp
from jax import lax
from jax.sharding import PartitionSpec as P

FINE_STEPS = 4
SWEEPS = 8
COARSE_SWEEPS = 2
ITERS = 2


stress_factor = 0.15
fine_size = 0.25


def next_rows(array):
    return jnp.concatenate([array[:, 1:, :], jnp.zeros_like(array[:, :1, :])], axis=1)


def prev_rows(array):
    return jnp.concatenate([jnp.zeros_like(array[:, :1, :]), array[:, :-1, :]], axis=1)


def next_cols(array):
    return jnp.concatenate([array[:, :, 1:], jnp.zeros_like(array[:, :, :1])], axis=2)


def prev_cols(array):
    return jnp.concatenate([jnp.zeros_like(array[:, :, :1]), array[:, :, :-1]], axis=2)


def implicit(pressure, slice_source, step_size, sweeps, fields, couple):
    storage, perm_base, leakoff, tisum = fields
    permeability = perm_base * jnp.exp(stress_factor * pressure)
    row_index = lax.broadcasted_iota(jnp.int32, pressure.shape, 1)
    col_index = lax.broadcasted_iota(jnp.int32, pressure.shape, 2)
    face_rows = jnp.where(
        row_index < pressure.shape[1] - 1, 0.5 * (permeability + next_rows(permeability)), 0.0
    )
    face_cols = jnp.where(
        col_index < pressure.shape[2] - 1, 0.5 * (permeability + next_cols(permeability)), 0.0
    )
    storage_rate = storage / step_size
    diagonal_total = (
        storage_rate + leakoff + face_rows + prev_rows(face_rows) + face_cols + prev_cols(face_cols)
    )
    right_side = storage_rate * pressure + slice_source
    if couple is not None:
        diagonal_total = diagonal_total + tisum
        right_side = right_side + couple(pressure)

    def sweep(sweep_index, current):
        beside = face_rows * next_rows(current) + prev_rows(face_rows * current)
        beside = beside + face_cols * next_cols(current) + prev_cols(face_cols * current)
        return (right_side + beside) / diagonal_total

    return lax.fori_loop(0, sweeps, sweep, pressure)


def body(
    pressure0,
    storage,
    perm_base,
    leakoff,
    sources,
    export_cells,
    inter_local,
    trace_source,
    inter_trans,
    inter_count,
):
    slice_count = lax.axis_size("tm")
    slice_index = lax.axis_index("tm")
    own_source = sources[0]
    entry_index = lax.broadcasted_iota(jnp.int32, inter_local.shape, 0)
    weights = jnp.where(entry_index < inter_count[0], inter_trans, jnp.zeros_like(inter_trans))
    cell_total = pressure0.size
    tisum = (
        jnp.zeros((cell_total,), jnp.float32).at[inter_local].add(weights).reshape(pressure0.shape)
    )
    fields = (storage, perm_base, leakoff, tisum)

    def couple(current):
        flat_field = current.reshape(-1)
        exported = flat_field[export_cells]
        gathered = lax.all_gather(exported, "frac", axis=0, tiled=True)
        remote_values = gathered[trace_source]
        return (
            jnp.zeros_like(flat_field)
            .at[inter_local]
            .add(weights * remote_values)
            .reshape(current.shape)
        )

    def coarse(pressure, slice_source):
        return implicit(pressure, slice_source, fine_size * FINE_STEPS, COARSE_SWEEPS, fields, None)

    all_sources = lax.all_gather(sources, "tm", axis=0, tiled=True)

    def chain(correction, carry_zero):
        if carry_zero:
            all_corrections = jnp.zeros_like(all_sources)
        else:
            all_corrections = lax.all_gather(correction[None], "tm", axis=0, tiled=True)

        def turn(turn_index, carried):
            current, kept_state = carried
            slice_source = lax.dynamic_index_in_dim(all_sources, turn_index, 0, keepdims=False)
            added = lax.dynamic_index_in_dim(all_corrections, turn_index, 0, keepdims=False)
            current = coarse(current, slice_source) + added
            kept_state = jnp.where(slice_index == turn_index + 1, current, kept_state)
            return (current, kept_state)

        final_pair = lax.fori_loop(0, slice_count - 1, turn, (pressure0, pressure0))
        return final_pair[1]

    state = chain(jnp.zeros_like(pressure0), True)
    for iteration in range(ITERS):
        fine_pressure = state
        for step_number in range(FINE_STEPS):
            fine_pressure = implicit(fine_pressure, own_source, fine_size, SWEEPS, fields, couple)
        coarse_end = coarse(state, own_source)
        state = chain(fine_pressure - coarse_end, False)
    return state[None]


def solution(mesh):
    placed = (
        P("frac", None, None),
        P("frac", None, None),
        P("frac", None, None),
        P("frac", None, None),
        P("tm", "frac", None, None),
        P("frac"),
        P("frac"),
        P("frac"),
        P("frac"),
        P("frac"),
    )
    return jax.shard_map(
        body, mesh=mesh, in_specs=placed, out_specs=P("tm", "frac", None, None), check_vma=False
    )
```

profile of v0, /device:TPU:448, one launch (start us, length us, event | category | flops | bytes accessed | tf_op | source)
XLA Modules:
  0.0 725.9 jit_solution(9327614761849319025)
XLA Ops:
  11.1 80.9 %all-gather.22.cloned.1.call-done = f32[32,4,32,128]{3,2,1,0:T(8,128)} async-done(((f32[1,4,32,128]{3,2,1,0:T(8,128)}), f32[32,4,32,128]{3,2,1,0:T(8,128)}) %all-gather.22.cloned.1.call-update) | async-done | bytes 2097168 | tf_op jit(solution)/shard_map/all_gather | solution.py:98
  92.1 52.9 %while.235 = (s32[]{:T(128)}, f32[4,32,128]{2,1,0:T(8,128)S(1)}, f32[4,32,128]{2,1,0:T(8,128)S(1)}, f32[4,32,128]{2,1,0:T(8,128)}, f32[4,32,128]{2,1,0:T(8,128)}...) while((s32[]{:T(128)}, f32[4,32,128]{2,1,0:T(8,128)S(1)}, ...), condition=%wide.region_3.4_spmd, body=%wide.region_0.3_spmd.sunk | while | flops 392741 | bytes 2790472 | solution.py:114
  95.5 0.9 bitcast_add_fusion.20
  146.0 1.7 gather_fusion
  147.7 17.0 %all-gather.10 = f32[16,1,256]{2,1,0:T(1,128)S(1)} all-gather(f32[1,1,256]{2,1,0:T(1,128)S(1)} %bitcast.174), channel_id=2, replica_groups=mesh['tm'=32,'frac'=16] {'frac'}, dimensions={0}, use_global_device_ids=true | all-gather | bytes 17408 | tf_op jit(solution)/shard_map/all_gather | solution.py:86
  164.7 6.1 gather_fusion.1
  170.9 5.9 scatter_custom_fusion.1
  176.8 5.9 scatter_custom_fusion
  183.0 1.7 while.236
  184.7 1.7 gather_fusion.2
  186.4 15.2 %all-gather.11 = f32[16,1,256]{2,1,0:T(1,128)S(1)} all-gather(f32[1,1,256]{2,1,0:T(1,128)S(1)} %bitcast.175), channel_id=3, replica_groups=mesh['tm'=32,'frac'=16] {'frac'}, dimensions={0}, use_global_device_ids=true | all-gather | bytes 17408 | tf_op jit(solution)/shard_map/all_gather | solution.py:86
  201.7 6.1 gather_fusion.3
  207.8 5.9 scatter_custom_fusion.2
  214.1 1.7 while.237
  215.8 1.7 gather_fusion.4
  217.5 15.1 %all-gather.12 = f32[16,1,256]{2,1,0:T(1,128)S(1)} all-gather(f32[1,1,256]{2,1,0:T(1,128)S(1)} %bitcast.176), channel_id=4, replica_groups=mesh['tm'=32,'frac'=16] {'frac'}, dimensions={0}, use_global_device_ids=true | all-gather | bytes 17408 | tf_op jit(solution)/shard_map/all_gather | solution.py:86
  232.6 6.1 gather_fusion.5
  238.8 5.9 scatter_custom_fusion.3
  245.1 1.7 while.238
  246.8 1.7 gather_fusion.6
  248.5 15.2 %all-gather.13 = f32[16,1,256]{2,1,0:T(1,128)S(1)} all-gather(f32[1,1,256]{2,1,0:T(1,128)S(1)} %bitcast.177), channel_id=5, replica_groups=mesh['tm'=32,'frac'=16] {'frac'}, dimensions={0}, use_global_device_ids=true | all-gather | bytes 17408 | tf_op jit(solution)/shard_map/all_gather | solution.py:86
  263.8 6.1 gather_fusion.7
  269.9 5.9 scatter_custom_fusion.4
  276.6 1.7 while.239
  279.3 78.6 %all-gather.24.cloned.1.call-done = f32[128,32,128]{2,1,0:T(8,128)} async-done(((f32[4,32,128]{2,1,0:T(8,128)}), f32[128,32,128]{2,1,0:T(8,128)}) %all-gather.24.cloned.1.call-update) | async-done | bytes 2097168 | tf_op jit(solution)/shard_map/all_gather | solution.py:104
  357.8 77.4 %while.242 = (s32[]{:T(128)}, f32[4,32,128]{2,1,0:T(8,128)S(1)}, f32[4,32,128]{2,1,0:T(8,128)S(1)}, f32[4,32,128]{2,1,0:T(8,128)S(1)}, f32[4,32,128]{2,1,0:T(8,1...) while((s32[]{:T(128)}, f32[4,32,128]{2,1,0:T(8,128)S(1)}, ...), condition=%wide.region_22.23_spmd, body=%wide.region_19.22_spmd.sunk | while | flops 409125 | bytes 2921564 | solution.py:114
  435.3 1.7 gather_fusion.8
  437.0 17.0 %all-gather.14 = f32[16,1,256]{2,1,0:T(1,128)S(1)} all-gather(f32[1,1,256]{2,1,0:T(1,128)S(1)} %bitcast.178), channel_id=7, replica_groups=mesh['tm'=32,'frac'=16] {'frac'}, dimensions={0}, use_global_device_ids=true | all-gather | bytes 17408 | tf_op jit(solution)/shard_map/all_gather | solution.py:86
  454.0 6.1 gather_fusion.9
  460.2 5.9 scatter_custom_fusion.5
  466.5 1.7 while.243
  468.2 1.7 gather_fusion.10
  469.9 15.2 %all-gather.15 = f32[16,1,256]{2,1,0:T(1,128)S(1)} all-gather(f32[1,1,256]{2,1,0:T(1,128)S(1)} %bitcast.179), channel_id=8, replica_groups=mesh['tm'=32,'frac'=16] {'frac'}, dimensions={0}, use_global_device_ids=true | all-gather | bytes 17408 | tf_op jit(solution)/shard_map/all_gather | solution.py:86
  485.1 6.1 gather_fusion.11
  491.3 5.9 scatter_custom_fusion.6
  497.6 1.7 while.244
  499.3 1.7 gather_fusion.12
  501.0 15.1 %all-gather.16 = f32[16,1,256]{2,1,0:T(1,128)S(1)} all-gather(f32[1,1,256]{2,1,0:T(1,128)S(1)} %bitcast.180), channel_id=9, replica_groups=mesh['tm'=32,'frac'=16] {'frac'}, dimensions={0}, use_global_device_ids=true | all-gather | bytes 17408 | tf_op jit(solution)/shard_map/all_gather | solution.py:86
  516.1 6.1 gather_fusion.13
  522.3 5.9 scatter_custom_fusion.7
  528.5 1.7 while.245
  530.3 1.7 gather_fusion.14
  532.0 15.2 %all-gather.17 = f32[16,1,256]{2,1,0:T(1,128)S(1)} all-gather(f32[1,1,256]{2,1,0:T(1,128)S(1)} %bitcast.173), channel_id=10, replica_groups=mesh['tm'=32,'frac'=16] {'frac'}, dimensions={0}, use_global_device_ids=true | all-gather | bytes 17408 | tf_op jit(solution)/shard_map/all_gather | solution.py:86
  547.2 6.1 gather_fusion.15
  553.4 5.9 scatter_custom_fusion.8
  560.1 1.7 while.246
  562.5 78.8 %all-gather.26.cloned.1.call-done = f32[128,32,128]{2,1,0:T(8,128)} async-done(((f32[4,32,128]{2,1,0:T(8,128)}), f32[128,32,128]{2,1,0:T(8,128)}) %all-gather.26.cloned.1.call-update) | async-done | bytes 2097168 | tf_op jit(solution)/shard_map/all_gather | solution.py:104
  641.3 77.4 %while.249 = (s32[]{:T(128)}, f32[4,32,128]{2,1,0:T(8,128)S(1)}, f32[4,32,128]{2,1,0:T(8,128)S(1)}, f32[4,32,128]{2,1,0:T(8,128)S(1)}, f32[4,32,128]{2,1,0:T(8,1...) while((s32[]{:T(128)}, f32[4,32,128]{2,1,0:T(8,128)S(1)}, ...), condition=%wide.region_40.41_spmd, body=%wide.region_37.40_spmd.sunk | while | flops 409125 | bytes 2921564 | solution.py:114
  (1683 shorter events, 260.9 us)
Async XLA Ops:
  6.5 85.5 %all-gather.22.cloned.1.call-start = ((), (), s32[]{:S(2)}) async-start(), calls=%async_computation | async-start | bytes 2162688 | tf_op jit(solution)/shard_map/all_gather | solution.py:98
  7.4 350.4 %all-gather.24.cloned.1.call-start = ((), (), s32[]{:S(2)}) async-start(), calls=%async_computation.1 | async-start | bytes 2162688 | tf_op jit(solution)/shard_map/all_gather | solution.py:104
  164.7 6.2 copy-start.5
  164.7 18.2 %copy-start = (f32[4,32,128]{2,1,0:T(8,128)S(1)}, f32[4,32,128]{2,1,0:T(8,128)}, u32[]{:S(2)}) copy-start(f32[4,32,128]{2,1,0:T(8,128)} %get-tuple-element.2573) | copy-start | bytes 196612
  164.7 18.2 %copy-start.2 = (f32[1,4,32,128]{3,2,1,0:T(8,128)S(1)}, f32[1,4,32,128]{3,2,1,0:T(8,128)}, u32[]{:S(2)}) copy-start(f32[1,4,32,128]{3,2,1,0:T(8,128)} %param.46) | copy-start | bytes 196612
  164.7 18.2 %copy-start.4 = (f32[4,32,128]{2,1,0:T(8,128)S(1)}, f32[4,32,128]{2,1,0:T(8,128)}, u32[]{:S(2)}) copy-start(f32[4,32,128]{2,1,0:T(8,128)} %param.45) | copy-start | bytes 196612
  201.7 12.1 %copy-start.1 = (f32[4,32,128]{2,1,0:T(8,128)S(1)}, f32[4,32,128]{2,1,0:T(8,128)}, u32[]{:S(2)}) copy-start(f32[4,32,128]{2,1,0:T(8,128)} %get-tuple-element.2579) | copy-start | bytes 196612
  279.0 362.3 %all-gather.26.cloned.1.call-start = ((), (), s32[]{:S(2)}) async-start(), calls=%async_computation.2 | async-start | bytes 2162688 | tf_op jit(solution)/shard_map/all_gather | solution.py:104
  718.8 0.6 copy-start.3
Sparse Core Ops, SparseCore 0:
  10.5 81.5 all-gather.21
  279.1 78.6 all-gather.23
  562.6 78.6 all-gather.25
where the time goes:
time: 741 us; the launch traced here: 726 us
  other arithmetic  264 us (36%)
  waiting for transfers between devices  238 us (32%)
  blocking collectives  125 us (17%)
  local copies, waits for them, and re-layouts  73.4 us (10%)
  between operations  14.4 us (2%)
  loops' own time  10.6 us (1%)
    all_gather x2, waiting for transfers between devices, chain(): all_corrections = lax.all_gather(correction[None], 'tm', axis=0, tiled=True)  157 us
    all_gather x8, blocking collectives, couple(): gathered = lax.all_gather(exported, 'frac', axis=0, tiled=True)  125 us
    add x94, other arithmetic, implicit(): right_side = storage_rate * pressure + slice_source  82.8 us
    all_gather x1, waiting for transfers between devices, body(): all_sources = lax.all_gather(sources, 'tm', axis=0, tiled=True)  80.9 us
    select_n x93, other arithmetic, turn(): kept_state = jnp.where(slice_index == turn_index + 1, current, kept_state)  55 us
    gather x8, local copies, waits for them, and re-layouts, couple(): remote_values = gathered[trace_source]  49.2 us
    scatter-add x8, other arithmetic, couple(): return jnp.zeros_like(flat_field).at[inter_local].add(weights * remote_va...  47.6 us
    div x254, other arithmetic, sweep(): return (right_side + beside) / diagonal_total  25 us
  transfers between devices with their start and end apart: 3, of which 3 were waited for; matrix products, arithmetic and copies ran while one was open for 0% of the time, Pallas kernels for 0%

commit v1 on v0

v1 whole, which is shorter than its diff:
```python
import functools

import jax
import jax.numpy as jnp
from jax import lax
from jax.experimental import pallas as pl
from jax.experimental.pallas import tpu as pltpu
from jax.sharding import PartitionSpec as P

FINE_STEPS = 4
SWEEPS = 8
COARSE_SWEEPS = 2
ITERS = 2
GROUP = 4

stress_factor = 0.15
fine_size = 0.25


def next_rows(v):
    return jnp.concatenate(
        [v[..., 1:, :, :], pltpu.roll(v[..., :1, :, :], 7, v.ndim - 2)], axis=v.ndim - 3
    )


def prev_rows(v):
    return jnp.concatenate(
        [pltpu.roll(v[..., 3:, :, :], 1, v.ndim - 2), v[..., :3, :, :]], axis=v.ndim - 3
    )


def next_cols(v):
    return pltpu.roll(v, 127, v.ndim - 1)


def prev_cols(v):
    return pltpu.roll(v, 1, v.ndim - 1)


def faces(pressure, perm):
    conductivity = perm * jnp.exp(stress_factor * pressure)
    shape = pressure.shape
    block = lax.broadcasted_iota(jnp.int32, shape, len(shape) - 3)
    sub = lax.broadcasted_iota(jnp.int32, shape, len(shape) - 2)
    lane = lax.broadcasted_iota(jnp.int32, shape, len(shape) - 1)
    row_half = jnp.where((block == 3) & (sub == 7), 0.0, 0.5)
    col_half = jnp.where(lane == 127, 0.0, 0.5)
    face_r = row_half * (conductivity + next_rows(conductivity))
    face_c = col_half * (conductivity + next_cols(conductivity))
    return face_r, prev_rows(face_r), face_c, prev_cols(face_c)


def sweep(v, base, weights):
    down, up, right, left = weights
    return base + (down * next_rows(v) + up * prev_rows(v)) + (
        right * next_cols(v) + left * prev_cols(v)
    )


def coarse(pressure, source, store, perm, leak):
    parts = faces(pressure, perm)
    inverse = 1.0 / (store + leak + (parts[0] + parts[1]) + (parts[2] + parts[3]))
    base = (store * pressure + source) * inverse
    weights = [part * inverse for part in parts]
    v = pressure
    for _ in range(COARSE_SWEEPS):
        v = sweep(v, base, weights)
    return v


def pick(table, lanes):
    return jnp.take_along_axis(table, lanes, axis=1, mode="promise_in_bounds")


def kernel(
    planes,
    peers,
    count_ref,
    pressure_ref,
    storage_ref,
    perm_ref,
    leak_ref,
    source_ref,
    export_ref,
    local_ref,
    trace_ref,
    trans_ref,
    out_ref,
    start,
    store,
    perm,
    leak,
    tisum,
    own_source,
    source_in,
    u_out,
    u_in,
    f_out,
    f_in,
    edge_in,
    edge_out,
    coarse_old,
    shared,
    field,
    row_hot,
    lane_hot,
    export_lane,
    export_code,
    trace_lane,
    trace_row,
    weight,
    source_send,
    source_recv,
    u_send,
    u_recv,
    f_send,
    f_recv,
    edge_send,
    edge_recv,
    share_send,
    share_recv,
):
    slice_index = lax.axis_index("tm")
    me = lax.axis_index("frac")
    plane = slice_index // GROUP
    column = slice_index % GROUP
    others = sorted(range(1, peers), key=lambda d: -min(d, peers - d))

    barrier = pltpu.get_barrier_semaphore()
    for d in others:
        pl.semaphore_signal(
            barrier, inc=1, device_id={"tm": slice_index, "frac": (me + d) % peers}
        )
    for d in range(1, GROUP):
        pl.semaphore_signal(
            barrier,
            inc=1,
            device_id={"tm": plane * GROUP + (column + d) % GROUP, "frac": me},
        )

    for d in (1, planes - 1):
        pl.semaphore_signal(
            barrier,
            inc=1,
            device_id={"tm": (plane + d) % planes * GROUP + column, "frac": me},
        )

    for f in range(GROUP):
        for r in range(4):
            rows = pl.ds(f * 32 + r, 8, stride=4)
            start[f, r] = pressure_ref[rows, :]
            store[f, r] = storage_ref[rows, :]
            perm[f, r] = perm_ref[rows, :]
            leak[f, r] = leak_ref[rows, :]
            own_source[f, r] = source_ref[rows, :]

    sub8 = lax.broadcasted_iota(jnp.int32, (8, 128), 0)
    lane8 = lax.broadcasted_iota(jnp.int32, (8, 128), 1)
    for g in range(2):
        cell = jnp.broadcast_to(export_ref[g : g + 1, :], (8, 128))
        row = (cell >> 7) & 31
        export_lane[g] = cell & 127
        export_code[g] = jnp.where((row >> 2) == sub8, (cell >> 12) * 4 + (row & 3), -1)
    slot = trace_ref[...]
    trace_lane[...] = slot & 127
    trace_row[...] = slot >> 7
    live = (sub8 * 128 + lane8) < count_ref[0]
    weight[...] = jnp.where(live, trans_ref[...], 0.0)
    cell = local_ref[...]
    cell_row = (cell >> 7) & 31
    code = (cell >> 12) * 32 + (cell_row & 3) * 8 + (cell_row >> 2)
    cell_lane = cell & 127
    number = lax.broadcasted_iota(jnp.int32, (128, 128), 0)
    for t in range(8):
        rows_t = jnp.broadcast_to(code[t : t + 1, :], (128, 128))
        row_hot[t] = jnp.where(rows_t == number, 1.0, 0.0).astype(jnp.bfloat16)
        lanes_t = jnp.broadcast_to(cell_lane[t : t + 1, :], (128, 128))
        hot = jnp.where(lanes_t == number, 1.0, 0.0)
        lane_hot[t * 128 : (t + 1) * 128, :] = hot.T.astype(jnp.bfloat16)

    def scatter(parts):
        total = jnp.zeros((128 * len(parts), 128), jnp.float32)
        for p in range(4):
            stacked = []
            for part in parts:
                pieces = []
                for t in (2 * p, 2 * p + 1):
                    line = jnp.broadcast_to(part[t : t + 1, :], (16, 128)).astype(jnp.bfloat16)
                    block = row_hot[t].reshape(8, 16, 128) * line[None]
                    pieces.append(block.reshape(128, 128))
                stacked.append(jnp.concatenate(pieces, axis=1))
            left = jnp.concatenate(stacked, axis=0)
            right = lane_hot[p * 256 : (p + 1) * 256, :]
            total = total + jnp.dot(left, right, preferred_element_type=jnp.float32)
        result = total[:128]
        for n in range(1, len(parts)):
            result = result + total[n * 128 : (n + 1) * 128]
        return result.reshape(GROUP, 4, 8, 128)

    def terms(value, number_of):
        parts = []
        for _ in range(number_of):
            part = value.astype(jnp.bfloat16).astype(jnp.float32)
            parts.append(part)
            value = value - part
        return parts

    tisum[...] = scatter(terms(weight[...], 3))

    pl.semaphore_wait(barrier, peers - 1 + GROUP - 1 + 2)

    def source_copy(target):
        return pltpu.make_async_remote_copy(
            src_ref=own_source.at[target],
            dst_ref=source_in.at[column],
            send_sem=source_send.at[target],
            recv_sem=source_recv.at[column],
            device_id={"tm": plane * GROUP + target, "frac": me},
        )

    def source_arrival(origin):
        return pltpu.make_async_remote_copy(
            src_ref=own_source.at[origin],
            dst_ref=source_in.at[origin],
            send_sem=source_send.at[origin],
            recv_sem=source_recv.at[origin],
            device_id={"tm": plane * GROUP + origin, "frac": me},
        )

    def u_copy(k, target):
        return pltpu.make_async_remote_copy(
            src_ref=u_out.at[k, target],
            dst_ref=u_in.at[k, column],
            send_sem=u_send.at[k, target],
            recv_sem=u_recv.at[k, column],
            device_id={"tm": plane * GROUP + target, "frac": me},
        )

    def u_arrival(k, origin):
        return pltpu.make_async_remote_copy(
            src_ref=u_out.at[k, origin],
            dst_ref=u_in.at[k, origin],
            send_sem=u_send.at[k, origin],
            recv_sem=u_recv.at[k, origin],
            device_id={"tm": plane * GROUP + origin, "frac": me},
        )

    def f_copy(k, target):
        return pltpu.make_async_remote_copy(
            src_ref=f_out.at[k, target],
            dst_ref=f_in.at[k, column],
            send_sem=f_send.at[k, target],
            recv_sem=f_recv.at[k, column],
            device_id={"tm": plane * GROUP + target, "frac": me},
        )

    def f_arrival(k, origin):
        return pltpu.make_async_remote_copy(
            src_ref=f_out.at[k, origin],
            dst_ref=f_in.at[k, origin],
            send_sem=f_send.at[k, origin],
            recv_sem=f_recv.at[k, origin],
            device_id={"tm": plane * GROUP + origin, "frac": me},
        )

    def edge_copy(k, target):
        return pltpu.make_async_remote_copy(
            src_ref=edge_out.at[k],
            dst_ref=edge_in.at[k],
            send_sem=edge_send.at[k],
            recv_sem=edge_recv.at[k],
            device_id={"tm": target, "frac": me},
        )

    def share_copy(m, target):
        return pltpu.make_async_remote_copy(
            src_ref=shared.at[m, me],
            dst_ref=shared.at[m, me],
            send_sem=share_send.at[m],
            recv_sem=share_recv.at[m],
            device_id={"tm": slice_index, "frac": target},
        )

    def share_all(m):
        return pltpu.make_async_remote_copy(
            src_ref=shared.at[m, pl.ds(0, peers - 1)],
            dst_ref=shared.at[m, pl.ds(0, peers - 1)],
            send_sem=share_send.at[m],
            recv_sem=share_recv.at[m],
            device_id={"tm": slice_index, "frac": (me + 1) % peers},
        )

    for d in range(1, GROUP):
        source_copy((column + d) % GROUP).start()
    source_in[column] = own_source[column]

    def chain(k, first):
        @pl.when(plane > 0)
        def _():
            edge_copy(k, slice_index - GROUP).wait_recv()

        @pl.when(plane == 0)
        def _():
            edge_in[k] = start[column]

        u = edge_in[k]
        for j in range(GROUP):
            u_out[k, j] = u

            @pl.when(column != j)
            def _():
                u_copy(k, j).start()
                if first:
                    source_arrival(j).wait_recv()
                else:
                    f_arrival(k - 1, j).wait_recv()

            following = coarse(u, source_in[j], store[column], perm[column], leak[column])
            if first:
                u = following
            else:
                u = following + (f_in[k - 1, j] - coarse_old[j])
            coarse_old[j] = following
        edge_out[k] = u

        @pl.when(plane < planes - 1)
        def _():
            edge_copy(k, slice_index + GROUP).start()

        u_in[k, column] = u_out[k, column]
        for d in range(1, GROUP):
            u_arrival(k, (column + d) % GROUP).wait_recv()

    def fine(k):
        field[...] = u_in[k]

        def step(t, carry):
            m = k * FINE_STEPS + t
            q = field[...]
            for g in range(2):
                lanes, codes = export_lane[g], export_code[g]
                found = jnp.zeros((8, 128), jnp.float32)
                for n in range(4 * GROUP):
                    found = jnp.where(codes == n, pick(q[n // 4, n % 4], lanes), found)
                shared[m, me, g : g + 1, :] = jnp.sum(found, axis=0, keepdims=True)
            for d in others:
                share_copy(m, (me + d) % peers).start()

            parts = faces(q, perm[...])
            rate = store[...] * (1.0 / fine_size)
            total = rate + leak[...] + tisum[...] + (parts[0] + parts[1]) + (parts[2] + parts[3])
            inverse = 1.0 / total
            base = (rate * q + own_source[...]) * inverse
            weights = [part * inverse for part in parts]

            share_all(m).wait_recv()
            rows = trace_row[...]
            lanes = trace_lane[...]
            value = jnp.zeros((8, 128), jnp.float32)
            for n in range(2 * peers):
                line = jnp.broadcast_to(shared[m, n // 2, n % 2 : n % 2 + 1, :], (8, 128))
                value = jnp.where(rows == n, pick(line, lanes), value)
            base = base + scatter(terms(weight[...] * value, 2)) * inverse
            v = q
            for _ in range(SWEEPS):
                v = sweep(v, base, weights)
            field[...] = v
            return carry

        lax.fori_loop(0, FINE_STEPS, step, 0)
        f_out[k] = field[...]
        for d in range(1, GROUP):
            f_copy(k, (column + d) % GROUP).start()
        f_in[k, column] = f_out[k, column]

    chain(0, True)

    def iteration(k, carry):
        fine(k)
        chain(k + 1, False)
        return carry

    lax.fori_loop(0, ITERS, iteration, 0)

    for f in range(GROUP):
        for r in range(4):
            out_ref[pl.ds(f * 32 + r, 8, stride=4), :] = u_in[ITERS, f, r]

    for d in range(1, GROUP):
        other = (column + d) % GROUP
        source_copy(other).wait_send()
        for k in range(ITERS + 1):
            u_copy(k, other).wait_send()
        for k in range(ITERS):
            f_copy(k, other).wait_send()

    @pl.when(plane < planes - 1)
    def _():
        for k in range(ITERS + 1):
            edge_copy(k, slice_index + GROUP).wait_send()

    for m in range(ITERS * FINE_STEPS):
        share_all(m).wait_send()


def body(
    pressure0,
    storage,
    perm_base,
    leakoff,
    sources,
    export_cells,
    inter_local,
    trace_source,
    inter_trans,
    inter_count,
):
    planes = lax.axis_size("tm") // GROUP
    peers = lax.axis_size("frac")
    flat = lambda a: a.reshape(128, 128)
    vmem = pl.BlockSpec(memory_space=pltpu.VMEM)
    f32 = jnp.float32
    block = (4, 8, 128)
    whole = (GROUP,) + block
    shares = ITERS * FINE_STEPS
    out = pl.pallas_call(
        functools.partial(kernel, planes, peers),
        out_shape=jax.ShapeDtypeStruct((128, 128), f32),
        in_specs=[pl.BlockSpec(memory_space=pltpu.SMEM)] + [vmem] * 9,
        out_specs=vmem,
        scratch_shapes=[
            pltpu.VMEM(whole, f32),
            pltpu.VMEM(whole, f32),
            pltpu.VMEM(whole, f32),
            pltpu.VMEM(whole, f32),
            pltpu.VMEM(whole, f32),
            pltpu.VMEM(whole, f32),
            pltpu.VMEM(whole, f32),
            pltpu.VMEM((ITERS + 1,) + whole, f32),
            pltpu.VMEM((ITERS + 1,) + whole, f32),
            pltpu.VMEM((ITERS,) + whole, f32),
            pltpu.VMEM((ITERS,) + whole, f32),
            pltpu.VMEM((ITERS + 1,) + block, f32),
            pltpu.VMEM((ITERS + 1,) + block, f32),
            pltpu.VMEM(whole, f32),
            pltpu.VMEM((shares, peers, 2, 128), f32),
            pltpu.VMEM(whole, f32),
            pltpu.VMEM((8, 128, 128), jnp.bfloat16),
            pltpu.VMEM((1024, 128), jnp.bfloat16),
            pltpu.VMEM((2, 8, 128), jnp.int32),
            pltpu.VMEM((2, 8, 128), jnp.int32),
            pltpu.VMEM((8, 128), jnp.int32),
            pltpu.VMEM((8, 128), jnp.int32),
            pltpu.VMEM((8, 128), f32),
            pltpu.SemaphoreType.DMA((GROUP,)),
            pltpu.SemaphoreType.DMA((GROUP,)),
            pltpu.SemaphoreType.DMA((ITERS + 1, GROUP)),
            pltpu.SemaphoreType.DMA((ITERS + 1, GROUP)),
            pltpu.SemaphoreType.DMA((ITERS, GROUP)),
            pltpu.SemaphoreType.DMA((ITERS, GROUP)),
            pltpu.SemaphoreType.DMA((ITERS + 1,)),
            pltpu.SemaphoreType.DMA((ITERS + 1,)),
            pltpu.SemaphoreType.DMA((shares,)),
            pltpu.SemaphoreType.DMA((shares,)),
        ],
        compiler_params=pltpu.CompilerParams(collective_id=0, has_side_effects=True),
        name="parareal",
    )(
        inter_count,
        flat(pressure0),
        flat(storage),
        flat(perm_base),
        flat(leakoff),
        flat(sources),
        export_cells.reshape(2, 128),
        inter_local.reshape(8, 128),
        trace_source.reshape(8, 128),
        inter_trans.reshape(8, 128),
    )
    return out.reshape(sources.shape)


def solution(mesh):
    placed = (
        P("frac", None, None),
        P("frac", None, None),
        P("frac", None, None),
        P("frac", None, None),
        P("tm", "frac", None, None),
        P("frac"),
        P("frac"),
        P("frac"),
        P("frac"),
        P("frac"),
    )
    return jax.shard_map(
        body, mesh=mesh, in_specs=placed, out_specs=P("tm", "frac", None, None), check_vma=False
    )
```

time: 741 us -> 100 us (0.13); the launches traced: 726 us -> 100 us
  other arithmetic: 264 us -> 0 us
  waiting for transfers between devices: 238 us -> 0 us
  blocking collectives: 125 us -> 0 us
  Pallas kernels: 0 us -> 97.9 us
  local copies, waits for them, and re-layouts: 73.4 us -> 1.47 us
  between operations: 14.4 us -> 0.66 us
  loops' own time: 10.6 us -> 0 us
    all_gather x3 -> x0, waiting for transfers between devices: 238 us -> none  [the longest x2 157 us: chain(): all_corrections = lax.all_gather(correction[None], 'tm', axis=0, tiled=True)]
    all_gather x8 -> x0, blocking collectives: 125 us -> none  [couple(): gathered = lax.all_gather(exported, 'frac', axis=0, tiled=True)]
    pallas_call x0 -> x1, Pallas kernels: none -> 97.9 us  [body(): pl.pallas_call(functools.partial(kernel, planes, peers), out_shape=jax.Sh...]
    add x202 -> x0, other arithmetic: 92.8 us -> none  [the longest x94 82.8 us: implicit(): right_side = storage_rate * pressure + slice_source]
    select_n x196 -> x0, other arithmetic: 64.2 us -> none  [the longest x93 55 us: turn(): kept_state = jnp.where(slice_index == turn_index + 1, current, kept_state)]
    gather x16 -> x0, local copies, waits for them, and re-layouts: 62.9 us -> none  [the longest x8 49.2 us: couple(): remote_values = gathered[trace_source]]
    scatter-add x9 -> x0, other arithmetic: 53.5 us -> none  [the longest x8 47.6 us: couple(): return jnp.zeros_like(flat_field).at[inter_local].add(weights * remote_va...]
    div x254 -> x0, other arithmetic: 25 us -> none  [sweep(): return (right_side + beside) / diagonal_total]
  transfers between devices with their start and end apart: 3 -> 0, of which waited for: 3 -> 0; matrix products, arithmetic and copies ran while one was open for 0% -> 0% of each run, Pallas kernels for 0% -> 0%
where the time goes in v1:
time: 100 us
  Pallas kernels  97.9 us (98%)
  local copies, waits for them, and re-layouts  1.47 us (1%)
    pallas_call x1, Pallas kernels, body(): pl.pallas_call(functools.partial(kernel, planes, peers), out_shape=jax.Sh...  97.9 us

profile of v1, /device:TPU:448, one launch (start us, length us, event | category | flops | bytes accessed | tf_op | source)
XLA Modules:
  0.0 100.0 jit_solution(11402341583640533068)
XLA Ops:
  0.7 97.9 %parareal.1 = f32[128,128]{1,0:T(8,128)} custom-call(s32[1]{0:T(128)S(6)} %copy.12.count_ref, f32[128,128]{1,0:T(8,128)} %bitcast.11, f32[128,128]{1,0:T(8,128)} %bitcast.12, f32[128,128]{1,0:T(8,128)} %bitcast.13, f32[128,128]{1,0:T(8,128)} %bitcast.14, f32[128,128]{1,0:T(8,128)} %bitcast.15, s32[2,128]{1,0:T(2,128)} %bitcast.19, s32[8,128]{1,0:T(8,128)} %bitcast.16, ...), custom_call_target="tpu_custom_call" | custom-call | tf_op jit(solution)/shard_map/parareal/pallas_call | solution.py:426
  98.5 1.5 %copy.13 = f32[1,4,32,128]{3,2,1,0:T(8,128)} copy(f32[1,4,32,128]{3,2,1,0:T(8,128)} %bitcast.10) | data formatting | bytes 131072

commit v2 on v1

--- a/solution.py
+++ b/solution.py
@@ -76,6 +76,16 @@
     planes,
     peers,
     count_ref,
+    pressure_hbm,
+    storage_hbm,
+    perm_hbm,
+    leak_hbm,
+    source_hbm,
+    export_hbm,
+    local_hbm,
+    trace_hbm,
+    trans_hbm,
+    out_ref,
     pressure_ref,
     storage_ref,
     perm_ref,
@@ -85,7 +95,6 @@
     local_ref,
     trace_ref,
     trans_ref,
-    out_ref,
     start,
     store,
     perm,
@@ -109,6 +118,7 @@
     trace_lane,
     trace_row,
     weight,
+    fetched,
     source_send,
     source_recv,
     u_send,
@@ -138,12 +148,42 @@
             device_id={"tm": plane * GROUP + (column + d) % GROUP, "frac": me},
         )
 
-    for d in (1, planes - 1):
+    for d in (1, 2, planes - 2, planes - 1):
         pl.semaphore_signal(
             barrier,
             inc=1,
             device_id={"tm": (plane + d) % planes * GROUP + column, "frac": me},
         )
+    for d in range(1, GROUP):
+        for p in (1, planes - 1):
+            pl.semaphore_signal(
+                barrier,
+                inc=1,
+                device_id={
+                    "tm": (plane + p) % planes * GROUP + (column + d) % GROUP,
+                    "frac": me,
+                },
+            )
+
+    pairs = (
+        (source_hbm, source_ref),
+        (pressure_hbm, pressure_ref),
+        (storage_hbm, storage_ref),
+        (perm_hbm, perm_ref),
+        (leak_hbm, leak_ref),
+        (export_hbm, export_ref),
+        (local_hbm, local_ref),
+        (trace_hbm, trace_ref),
+        (trans_hbm, trans_ref),
+    )
+    fetches = [
+        pltpu.make_async_copy(origin, target, fetched.at[n])
+        for n, (origin, target) in enumerate(pairs)
+    ]
+    for fetch in fetches:
+        fetch.start()
+    for fetch in fetches:
+        fetch.wait()
 
     for f in range(GROUP):
         for r in range(4):
@@ -207,24 +247,25 @@
 
     tisum[...] = scatter(terms(weight[...], 3))
 
-    pl.semaphore_wait(barrier, peers - 1 + GROUP - 1 + 2)
-
-    def source_copy(target):
+    pl.semaphore_wait(barrier, peers - 1 + GROUP - 1 + 4 + 2 * (GROUP - 1))
+
+    def source_copy(ahead, target):
+        slot = (1 - ahead) * GROUP + column
         return pltpu.make_async_remote_copy(
             src_ref=own_source.at[target],
-            dst_ref=source_in.at[column],
-            send_sem=source_send.at[target],
-            recv_sem=source_recv.at[column],
-            device_id={"tm": plane * GROUP + target, "frac": me},
-        )
-
-    def source_arrival(origin):
-        return pltpu.make_async_remote_copy(
-            src_ref=own_source.at[origin],
-            dst_ref=source_in.at[origin],
-            send_sem=source_send.at[origin],
-            recv_sem=source_recv.at[origin],
-            device_id={"tm": plane * GROUP + origin, "frac": me},
+            dst_ref=source_in.at[slot],
+            send_sem=source_send.at[ahead, target],
+            recv_sem=source_recv.at[slot],
+            device_id={"tm": (plane + ahead) * GROUP + target, "frac": me},
+        )
+
+    def source_arrival(slot):
+        return pltpu.make_async_remote_copy(
+            src_ref=own_source.at[0],
+            dst_ref=source_in.at[slot],
+            send_sem=source_send.at[0, 0],
+            recv_sem=source_recv.at[slot],
+            device_id={"tm": plane * GROUP + (column + 1) % GROUP, "frac": me},
         )
 
     def u_copy(k, target):
@@ -245,22 +286,23 @@
             device_id={"tm": plane * GROUP + origin, "frac": me},
         )
 
-    def f_copy(k, target):
+    def f_copy(k, ahead, target):
+        slot = (1 - ahead) * GROUP + column
         return pltpu.make_async_remote_copy(
             src_ref=f_out.at[k, target],
-            dst_ref=f_in.at[k, column],
-            send_sem=f_send.at[k, target],
-            recv_sem=f_recv.at[k, column],
-            device_id={"tm": plane * GROUP + target, "frac": me},
-        )
-
-    def f_arrival(k, origin):
-        return pltpu.make_async_remote_copy(
-            src_ref=f_out.at[k, origin],
-            dst_ref=f_in.at[k, origin],
-            send_sem=f_send.at[k, origin],
-            recv_sem=f_recv.at[k, origin],
-            device_id={"tm": plane * GROUP + origin, "frac": me},
+            dst_ref=f_in.at[k, slot],
+            send_sem=f_send.at[k, ahead, target],
+            recv_sem=f_recv.at[k, slot],
+            device_id={"tm": (plane + ahead) * GROUP + target, "frac": me},
+        )
+
+    def f_arrival(k, slot):
+        return pltpu.make_async_remote_copy(
+            src_ref=f_out.at[k, 0],
+            dst_ref=f_in.at[k, slot],
+            send_sem=f_send.at[k, 0, 0],
+            recv_sem=f_recv.at[k, slot],
+            device_id={"tm": plane * GROUP + (column + 1) % GROUP, "frac": me},
         )
 
     def edge_copy(k, target):
@@ -290,18 +332,46 @@
             device_id={"tm": slice_index, "frac": (me + 1) % peers},
         )
 
-    for d in range(1, GROUP):
-        source_copy((column + d) % GROUP).start()
-    source_in[column] = own_source[column]
+    @pl.when(plane < planes - 1)
+    def _():
+        for d in (2, 1, 3, 0):
+            source_copy(1, (column + d) % GROUP).start()
+
+    for d in (2, 1, 3):
+        source_copy(0, (column + d) % GROUP).start()
+    source_in[GROUP + column] = own_source[column]
+
+    def advance(k, first, slot, u):
+        following = coarse(u, source_in[slot], store[column], perm[column], leak[column])
+        if first:
+            u = following
+        else:
+            u = following + (f_in[k - 1, slot] - coarse_old[slot])
+        coarse_old[slot] = following
+        return u
+
+    def arrival(k, first, slot):
+        if first:
+            source_arrival(slot).wait_recv()
+        else:
+            f_arrival(k - 1, slot).wait_recv()
 
     def chain(k, first):
+        @pl.when(plane > 1)
+        def _():
+            edge_copy(k, slice_index - 2 * GROUP).wait_recv()
+
+        @pl.when(plane <= 1)
+        def _():
+            edge_in[k] = start[column]
+
         @pl.when(plane > 0)
         def _():
-            edge_copy(k, slice_index - GROUP).wait_recv()
-
-        @pl.when(plane == 0)
-        def _():
-            edge_in[k] = start[column]
+            u = edge_in[k]
+            for j in range(GROUP):
+                arrival(k, first, j)
+                u = advance(k, first, j, u)
+            edge_in[k] = u
 
         u = edge_in[k]
         for j in range(GROUP):
@@ -310,22 +380,14 @@
             @pl.when(column != j)
             def _():
                 u_copy(k, j).start()
-                if first:
-                    source_arrival(j).wait_recv()
-                else:
-                    f_arrival(k - 1, j).wait_recv()
-
-            following = coarse(u, source_in[j], store[column], perm[column], leak[column])
-            if first:
-                u = following
-            else:
-                u = following + (f_in[k - 1, j] - coarse_old[j])
-            coarse_old[j] = following
+                arrival(k, first, GROUP + j)
+
+            u = advance(k, first, GROUP + j, u)
         edge_out[k] = u
 
-        @pl.when(plane < planes - 1)
+        @pl.when(plane < planes - 2)
         def _():
-            edge_copy(k, slice_index + GROUP).start()
+            edge_copy(k, slice_index + 2 * GROUP).start()
 
         u_in[k, column] = u_out[k, column]
         for d in range(1, GROUP):
@@ -369,9 +431,15 @@
 
         lax.fori_loop(0, FINE_STEPS, step, 0)
         f_out[k] = field[...]
-        for d in range(1, GROUP):
-            f_copy(k, (column + d) % GROUP).start()
-        f_in[k, column] = f_out[k, column]
+
+        @pl.when(plane < planes - 1)
+        def _():
+            for d in (2, 1, 3, 0):
+                f_copy(k, 1, (column + d) % GROUP).start()
+
+        for d in (2, 1, 3):
+            f_copy(k, 0, (column + d) % GROUP).start()
+        f_in[k, GROUP + column] = f_out[k, column]
 
     chain(0, True)
 
@@ -388,16 +456,23 @@
 
     for d in range(1, GROUP):
         other = (column + d) % GROUP
-        source_copy(other).wait_send()
+        source_copy(0, other).wait_send()
         for k in range(ITERS + 1):
             u_copy(k, other).wait_send()
         for k in range(ITERS):
-            f_copy(k, other).wait_send()
+            f_copy(k, 0, other).wait_send()
 
     @pl.when(plane < planes - 1)
     def _():
+        for f in range(GROUP):
+            source_copy(1, f).wait_send()
+            for k in range(ITERS):
+                f_copy(k, 1, f).wait_send()
+
+    @pl.when(plane < planes - 2)
+    def _():
         for k in range(ITERS + 1):
-            edge_copy(k, slice_index + GROUP).wait_send()
+            edge_copy(k, slice_index + 2 * GROUP).wait_send()
 
     for m in range(ITERS * FINE_STEPS):
         share_all(m).wait_send()
@@ -423,26 +498,37 @@
     block = (4, 8, 128)
     whole = (GROUP,) + block
     shares = ITERS * FINE_STEPS
+    slots = 2 * GROUP
     out = pl.pallas_call(
         functools.partial(kernel, planes, peers),
         out_shape=jax.ShapeDtypeStruct((128, 128), f32),
-        in_specs=[pl.BlockSpec(memory_space=pltpu.SMEM)] + [vmem] * 9,
+        in_specs=[pl.BlockSpec(memory_space=pltpu.SMEM)]
+        + [pl.BlockSpec(memory_space=pl.ANY)] * 9,
         out_specs=vmem,
         scratch_shapes=[
-            pltpu.VMEM(whole, f32),
-            pltpu.VMEM(whole, f32),
-            pltpu.VMEM(whole, f32),
-            pltpu.VMEM(whole, f32),
-            pltpu.VMEM(whole, f32),
-            pltpu.VMEM(whole, f32),
-            pltpu.VMEM(whole, f32),
+            pltpu.VMEM((128, 128), f32),
+            pltpu.VMEM((128, 128), f32),
+            pltpu.VMEM((128, 128), f32),
+            pltpu.VMEM((128, 128), f32),
+            pltpu.VMEM((128, 128), f32),
+            pltpu.VMEM((2, 128), jnp.int32),
+            pltpu.VMEM((8, 128), jnp.int32),
+            pltpu.VMEM((8, 128), jnp.int32),
+            pltpu.VMEM((8, 128), f32),
+            pltpu.VMEM(whole, f32),
+            pltpu.VMEM(whole, f32),
+            pltpu.VMEM(whole, f32),
+            pltpu.VMEM(whole, f32),
+            pltpu.VMEM(whole, f32),
+            pltpu.VMEM(whole, f32),
+            pltpu.VMEM((slots,) + block, f32),
             pltpu.VMEM((ITERS + 1,) + whole, f32),
             pltpu.VMEM((ITERS + 1,) + whole, f32),
             pltpu.VMEM((ITERS,) + whole, f32),
-            pltpu.VMEM((ITERS,) + whole, f32),
+            pltpu.VMEM((ITERS, slots) + block, f32),
             pltpu.VMEM((ITERS + 1,) + block, f32),
             pltpu.VMEM((ITERS + 1,) + block, f32),
-            pltpu.VMEM(whole, f32),
+            pltpu.VMEM((slots,) + block, f32),
             pltpu.VMEM((shares, peers, 2, 128), f32),
             pltpu.VMEM(whole, f32),
             pltpu.VMEM((8, 128, 128), jnp.bfloat16),
@@ -452,18 +538,21 @@
             pltpu.VMEM((8, 128), jnp.int32),
             pltpu.VMEM((8, 128), jnp.int32),
             pltpu.VMEM((8, 128), f32),
-            pltpu.SemaphoreType.DMA((GROUP,)),
-            pltpu.SemaphoreType.DMA((GROUP,)),
+            pltpu.SemaphoreType.DMA((9,)),
+            pltpu.SemaphoreType.DMA((2, GROUP)),
+            pltpu.SemaphoreType.DMA((slots,)),
             pltpu.SemaphoreType.DMA((ITERS + 1, GROUP)),
             pltpu.SemaphoreType.DMA((ITERS + 1, GROUP)),
-            pltpu.SemaphoreType.DMA((ITERS, GROUP)),
-            pltpu.SemaphoreType.DMA((ITERS, GROUP)),
+            pltpu.SemaphoreType.DMA((ITERS, 2, GROUP)),
+            pltpu.SemaphoreType.DMA((ITERS, slots)),
             pltpu.SemaphoreType.DMA((ITERS + 1,)),
             pltpu.SemaphoreType.DMA((ITERS + 1,)),
             pltpu.SemaphoreType.DMA((shares,)),
             pltpu.SemaphoreType.DMA((shares,)),
         ],
-        compiler_params=pltpu.CompilerParams(collective_id=0, has_side_effects=True),
+        compiler_params=pltpu.CompilerParams(
+            collective_id=0, has_side_effects=True
+        ),
         name="parareal",
     )(
         inter_count,

time: 100 us -> 93.2 us (0.932)
  Pallas kernels: 97.9 us -> 90.8 us
    pallas_call x1, Pallas kernels: 97.9 us -> 90.8 us  [body(): pl.pallas_call(functools.partial(kernel, planes, peers), out_shape=jax.Sh...]
where the time goes in v2:
time: 93.2 us; the launch traced here: 92.9 us
  Pallas kernels  90.8 us (97%)
  local copies, waits for them, and re-layouts  1.47 us (2%)
    pallas_call x1, Pallas kernels, body(): pl.pallas_call(functools.partial(kernel, planes, peers), out_shape=jax.Sh...  90.8 us

profile of v2, /device:TPU:448, one launch (start us, length us, event | category | flops | bytes accessed | tf_op | source)
XLA Modules:
  0.0 92.9 jit_solution(13249198456376515798)
XLA Ops:
  0.7 90.8 %parareal.1 = f32[128,128]{1,0:T(8,128)} custom-call(s32[1]{0:T(128)S(6)} %copy.12.count_ref, f32[128,128]{1,0:T(8,128)} %bitcast.11, f32[128,128]{1,0:T(8,128)} %bitcast.12, f32[128,128]{1,0:T(8,128)} %bitcast.13, f32[128,128]{1,0:T(8,128)} %bitcast.14, f32[128,128]{1,0:T(8,128)} %bitcast.15, s32[2,128]{1,0:T(2,128)} %bitcast.19, s32[8,128]{1,0:T(8,128)} %bitcast.16, ...), custom_call_target="tpu_custom_call" | custom-call | tf_op jit(solution)/shard_map/parareal/pallas_call | solution.py:502
  91.5 1.5 %copy.13 = f32[1,4,32,128]{3,2,1,0:T(8,128)} copy(f32[1,4,32,128]{3,2,1,0:T(8,128)} %bitcast.10) | data formatting | bytes 131072

commit v3 on v2

--- a/solution.py
+++ b/solution.py
@@ -109,7 +109,10 @@
     edge_in,
     edge_out,
     coarse_old,
+    first_out,
+    first_in,
     shared,
+    gathered,
     field,
     row_hot,
     lane_hot,
@@ -127,6 +130,8 @@
     f_recv,
     edge_send,
     edge_recv,
+    first_send,
+    first_recv,
     share_send,
     share_recv,
 ):
@@ -314,6 +319,24 @@
             device_id={"tm": target, "frac": me},
         )
 
+    def first_copy(k, target, peer):
+        return pltpu.make_async_remote_copy(
+            src_ref=first_out.at[k, target],
+            dst_ref=first_in.at[k, column * peers + me],
+            send_sem=first_send.at[k],
+            recv_sem=first_recv.at[k],
+            device_id={"tm": plane * GROUP + target, "frac": peer},
+        )
+
+    def first_all(k):
+        return pltpu.make_async_remote_copy(
+            src_ref=first_in.at[k, pl.ds(0, GROUP * peers - 1)],
+            dst_ref=first_in.at[k, pl.ds(0, GROUP * peers - 1)],
+            send_sem=first_send.at[k],
+            recv_sem=first_recv.at[k],
+            device_id={"tm": slice_index, "frac": (me + 1) % peers},
+        )
+
     def share_copy(m, target):
         return pltpu.make_async_remote_copy(
             src_ref=shared.at[m, me],
@@ -340,6 +363,32 @@
     for d in (2, 1, 3):
         source_copy(0, (column + d) % GROUP).start()
     source_in[GROUP + column] = own_source[column]
+
+    def exports(blocks, offset, g):
+        lanes, codes = export_lane[g], export_code[g] - offset
+        found = jnp.zeros((8, 128), jnp.float32)
+        for n in range(4 * blocks.shape[0]):
+            found = jnp.where(codes == n, pick(blocks[n // 4, n % 4], lanes), found)
+        return jnp.sum(found, axis=0, keepdims=True)
+
+    def announce(k):
+        for j in range(GROUP):
+            u = u_out[k, j][None]
+            for g in range(2):
+                first_out[k, j, g : g + 1, :] = exports(u, 4 * column, g)
+
+        def send(i, carry):
+            d = (peers // 2 + (1 - 2 * (i % 2)) * ((i + 1) // 2)) % peers
+            for j in range(GROUP):
+
+                @pl.when((d != 0) | (column != j))
+                def _():
+                    first_copy(k, j, (me + d) % peers).start()
+
+            return carry
+
+        lax.fori_loop(0, peers, send, 0)
+        first_in[k, column * peers + me] = first_out[k, column]
 
     def advance(k, first, slot, u):
         following = coarse(u, source_in[slot], store[column], perm[column], leak[column])
@@ -389,6 +438,14 @@
         def _():
             edge_copy(k, slice_index + 2 * GROUP).start()
 
+        if first:
+            announce(k)
+        else:
+
+            @pl.when(k < ITERS)
+            def _():
+                announce(k)
+
         u_in[k, column] = u_out[k, column]
         for d in range(1, GROUP):
             u_arrival(k, (column + d) % GROUP).wait_recv()
@@ -397,16 +454,15 @@
         field[...] = u_in[k]
 
         def step(t, carry):
-            m = k * FINE_STEPS + t
+            m = k * (FINE_STEPS - 1) + t - 1
             q = field[...]
-            for g in range(2):
-                lanes, codes = export_lane[g], export_code[g]
-                found = jnp.zeros((8, 128), jnp.float32)
-                for n in range(4 * GROUP):
-                    found = jnp.where(codes == n, pick(q[n // 4, n % 4], lanes), found)
-                shared[m, me, g : g + 1, :] = jnp.sum(found, axis=0, keepdims=True)
-            for d in others:
-                share_copy(m, (me + d) % peers).start()
+
+            @pl.when(t > 0)
+            def _():
+                for g in range(2):
+                    shared[m, me, g : g + 1, :] = exports(q, 0, g)
+                for d in others:
+                    share_copy(m, (me + d) % peers).start()
 
             parts = faces(q, perm[...])
             rate = store[...] * (1.0 / fine_size)
@@ -415,12 +471,24 @@
             base = (rate * q + own_source[...]) * inverse
             weights = [part * inverse for part in parts]
 
-            share_all(m).wait_recv()
+            @pl.when(t > 0)
+            def _():
+                share_all(m).wait_recv()
+                gathered[...] = shared[m]
+
+            @pl.when(t == 0)
+            def _():
+                first_all(k).wait_recv()
+                total = first_in[k, 0:peers]
+                for f in range(1, GROUP):
+                    total = total + first_in[k, f * peers : (f + 1) * peers]
+                gathered[...] = total
+
             rows = trace_row[...]
             lanes = trace_lane[...]
             value = jnp.zeros((8, 128), jnp.float32)
             for n in range(2 * peers):
-                line = jnp.broadcast_to(shared[m, n // 2, n % 2 : n % 2 + 1, :], (8, 128))
+                line = jnp.broadcast_to(gathered[n // 2, n % 2 : n % 2 + 1, :], (8, 128))
                 value = jnp.where(rows == n, pick(line, lanes), value)
             base = base + scatter(terms(weight[...] * value, 2)) * inverse
             v = q
@@ -474,7 +542,9 @@
         for k in range(ITERS + 1):
             edge_copy(k, slice_index + 2 * GROUP).wait_send()
 
-    for m in range(ITERS * FINE_STEPS):
+    for k in range(ITERS):
+        first_all(k).wait_send()
+    for m in range(ITERS * (FINE_STEPS - 1)):
         share_all(m).wait_send()
 
 
@@ -497,7 +567,7 @@
     f32 = jnp.float32
     block = (4, 8, 128)
     whole = (GROUP,) + block
-    shares = ITERS * FINE_STEPS
+    shares = ITERS * (FINE_STEPS - 1)
     slots = 2 * GROUP
     out = pl.pallas_call(
         functools.partial(kernel, planes, peers),
@@ -529,7 +599,10 @@
             pltpu.VMEM((ITERS + 1,) + block, f32),
             pltpu.VMEM((ITERS + 1,) + block, f32),
             pltpu.VMEM((slots,) + block, f32),
+            pltpu.VMEM((ITERS, GROUP, 2, 128), f32),
+            pltpu.VMEM((ITERS, GROUP * peers, 2, 128), f32),
             pltpu.VMEM((shares, peers, 2, 128), f32),
+            pltpu.VMEM((peers, 2, 128), f32),
             pltpu.VMEM(whole, f32),
             pltpu.VMEM((8, 128, 128), jnp.bfloat16),
             pltpu.VMEM((1024, 128), jnp.bfloat16),
@@ -547,6 +620,8 @@
             pltpu.SemaphoreType.DMA((ITERS, slots)),
             pltpu.SemaphoreType.DMA((ITERS + 1,)),
             pltpu.SemaphoreType.DMA((ITERS + 1,)),
+            pltpu.SemaphoreType.DMA((ITERS,)),
+            pltpu.SemaphoreType.DMA((ITERS,)),
             pltpu.SemaphoreType.DMA((shares,)),
             pltpu.SemaphoreType.DMA((shares,)),
         ],

time: 93.2 us -> 91.2 us (0.979)
  Pallas kernels: 90.8 us -> 88.9 us
    pallas_call x1, Pallas kernels: 90.8 us -> 88.9 us  [body(): pl.pallas_call(functools.partial(kernel, planes, peers), out_shape=jax.Sh...]
where the time goes in v3:
time: 91.2 us; the launch traced here: 91 us
  Pallas kernels  88.9 us (97%)
  local copies, waits for them, and re-layouts  1.47 us (2%)
    pallas_call x1, Pallas kernels, body(): pl.pallas_call(functools.partial(kernel, planes, peers), out_shape=jax.Sh...  88.9 us

profile of v3, /device:TPU:448, one launch (start us, length us, event | category | flops | bytes accessed | tf_op | source)
XLA Modules:
  0.0 91.0 jit_solution(5646073553348311638)
XLA Ops:
  0.7 88.9 %parareal.1 = f32[128,128]{1,0:T(8,128)} custom-call(s32[1]{0:T(128)S(6)} %copy.12.count_ref, f32[128,128]{1,0:T(8,128)} %bitcast.11, f32[128,128]{1,0:T(8,128)} %bitcast.12, f32[128,128]{1,0:T(8,128)} %bitcast.13, f32[128,128]{1,0:T(8,128)} %bitcast.14, f32[128,128]{1,0:T(8,128)} %bitcast.15, s32[2,128]{1,0:T(2,128)} %bitcast.19, s32[8,128]{1,0:T(8,128)} %bitcast.16, ...), custom_call_target="tpu_custom_call" | custom-call | tf_op jit(solution)/shard_map/parareal/pallas_call | solution.py:572
  89.6 1.5 %copy.13 = f32[1,4,32,128]{3,2,1,0:T(8,128)} copy(f32[1,4,32,128]{3,2,1,0:T(8,128)} %bitcast.10) | data formatting | bytes 131072

commit v4 on v3

--- a/solution.py
+++ b/solution.py
@@ -139,6 +139,8 @@
     me = lax.axis_index("frac")
     plane = slice_index // GROUP
     column = slice_index % GROUP
+    odd = plane % 2
+    partner = plane + 1 - 2 * odd
     others = sorted(range(1, peers), key=lambda d: -min(d, peers - d))
 
     barrier = pltpu.get_barrier_semaphore()
@@ -160,15 +162,11 @@
             device_id={"tm": (plane + d) % planes * GROUP + column, "frac": me},
         )
     for d in range(1, GROUP):
-        for p in (1, planes - 1):
-            pl.semaphore_signal(
-                barrier,
-                inc=1,
-                device_id={
-                    "tm": (plane + p) % planes * GROUP + (column + d) % GROUP,
-                    "frac": me,
-                },
-            )
+        pl.semaphore_signal(
+            barrier,
+            inc=1,
+            device_id={"tm": partner * GROUP + (column + d) % GROUP, "frac": me},
+        )
 
     pairs = (
         (source_hbm, source_ref),
@@ -252,7 +250,7 @@
 
     tisum[...] = scatter(terms(weight[...], 3))
 
-    pl.semaphore_wait(barrier, peers - 1 + GROUP - 1 + 4 + 2 * (GROUP - 1))
+    pl.semaphore_wait(barrier, peers - 1 + 2 * (GROUP - 1) + 4)
 
     def source_copy(ahead, target):
         slot = (1 - ahead) * GROUP + column
@@ -310,13 +308,22 @@
             device_id={"tm": plane * GROUP + (column + 1) % GROUP, "frac": me},
         )
 
-    def edge_copy(k, target):
+    def edge_copy(k, ahead):
         return pltpu.make_async_remote_copy(
             src_ref=edge_out.at[k],
             dst_ref=edge_in.at[k],
-            send_sem=edge_send.at[k],
+            send_sem=edge_send.at[k, ahead - 1],
             recv_sem=edge_recv.at[k],
-            device_id={"tm": target, "frac": me},
+            device_id={"tm": slice_index + ahead * GROUP, "frac": me},
+        )
+
+    def edge_arrival(k):
+        return pltpu.make_async_remote_copy(
+            src_ref=edge_out.at[k],
+            dst_ref=edge_in.at[k],
+            send_sem=edge_send.at[k, 0],
+            recv_sem=edge_recv.at[k],
+            device_id={"tm": slice_index - GROUP, "frac": me},
         )
 
     def first_copy(k, target, peer):
@@ -355,7 +362,7 @@
             device_id={"tm": slice_index, "frac": (me + 1) % peers},
         )
 
-    @pl.when(plane < planes - 1)
+    @pl.when(odd == 0)
     def _():
         for d in (2, 1, 3, 0):
             source_copy(1, (column + d) % GROUP).start()
@@ -377,17 +384,11 @@
             for g in range(2):
                 first_out[k, j, g : g + 1, :] = exports(u, 4 * column, g)
 
-        def send(i, carry):
-            d = (peers // 2 + (1 - 2 * (i % 2)) * ((i + 1) // 2)) % peers
+        for d in others:
             for j in range(GROUP):
-
-                @pl.when((d != 0) | (column != j))
-                def _():
-                    first_copy(k, j, (me + d) % peers).start()
-
-            return carry
-
-        lax.fori_loop(0, peers, send, 0)
+                first_copy(k, j, (me + d) % peers).start()
+        for d in range(1, GROUP):
+            first_copy(k, (column + d) % GROUP, me).start()
         first_in[k, column * peers + me] = first_out[k, column]
 
     def advance(k, first, slot, u):
@@ -408,13 +409,13 @@
     def chain(k, first):
         @pl.when(plane > 1)
         def _():
-            edge_copy(k, slice_index - 2 * GROUP).wait_recv()
+            edge_arrival(k).wait_recv()
 
         @pl.when(plane <= 1)
         def _():
             edge_in[k] = start[column]
 
-        @pl.when(plane > 0)
+        @pl.when(odd == 1)
         def _():
             u = edge_in[k]
             for j in range(GROUP):
@@ -434,9 +435,10 @@
             u = advance(k, first, GROUP + j, u)
         edge_out[k] = u
 
-        @pl.when(plane < planes - 2)
+        @pl.when((odd == 1) & (plane < planes - 2))
         def _():
-            edge_copy(k, slice_index + 2 * GROUP).start()
+            edge_copy(k, 2).start()
+            edge_copy(k, 1).start()
 
         if first:
             announce(k)
@@ -500,7 +502,7 @@
         lax.fori_loop(0, FINE_STEPS, step, 0)
         f_out[k] = field[...]
 
-        @pl.when(plane < planes - 1)
+        @pl.when(odd == 0)
         def _():
             for d in (2, 1, 3, 0):
                 f_copy(k, 1, (column + d) % GROUP).start()
@@ -530,17 +532,18 @@
         for k in range(ITERS):
             f_copy(k, 0, other).wait_send()
 
-    @pl.when(plane < planes - 1)
+    @pl.when(odd == 0)
     def _():
         for f in range(GROUP):
             source_copy(1, f).wait_send()
             for k in range(ITERS):
                 f_copy(k, 1, f).wait_send()
 
-    @pl.when(plane < planes - 2)
+    @pl.when((odd == 1) & (plane < planes - 2))
     def _():
         for k in range(ITERS + 1):
-            edge_copy(k, slice_index + 2 * GROUP).wait_send()
+            for ahead in (1, 2):
+                edge_copy(k, ahead).wait_send()
 
     for k in range(ITERS):
         first_all(k).wait_send()
@@ -618,7 +621,7 @@
             pltpu.SemaphoreType.DMA((ITERS + 1, GROUP)),
             pltpu.SemaphoreType.DMA((ITERS, 2, GROUP)),
             pltpu.SemaphoreType.DMA((ITERS, slots)),
-            pltpu.SemaphoreType.DMA((ITERS + 1,)),
+            pltpu.SemaphoreType.DMA((ITERS + 1, 2)),
             pltpu.SemaphoreType.DMA((ITERS + 1,)),
             pltpu.SemaphoreType.DMA((ITERS,)),
             pltpu.SemaphoreType.DMA((ITERS,)),

time: 91.2 us -> 89.8 us (0.985)
  Pallas kernels: 88.9 us -> 87.5 us
    pallas_call x1, Pallas kernels: 88.9 us -> 87.5 us  [body(): pl.pallas_call(functools.partial(kernel, planes, peers), out_shape=jax.Sh...]
where the time goes in v4:
time: 89.8 us; the launch traced here: 89.6 us
  Pallas kernels  87.5 us (97%)
  local copies, waits for them, and re-layouts  1.47 us (2%)
    pallas_call x1, Pallas kernels, body(): pl.pallas_call(functools.partial(kernel, planes, peers), out_shape=jax.Sh...  87.5 us

profile of v4, /device:TPU:448, one launch (start us, length us, event | category | flops | bytes accessed | tf_op | source)
XLA Modules:
  0.0 89.6 jit_solution(11815304776948377879)
XLA Ops:
  0.7 87.5 %parareal.1 = f32[128,128]{1,0:T(8,128)} custom-call(s32[1]{0:T(128)S(6)} %copy.12.count_ref, f32[128,128]{1,0:T(8,128)} %bitcast.11, f32[128,128]{1,0:T(8,128)} %bitcast.12, f32[128,128]{1,0:T(8,128)} %bitcast.13, f32[128,128]{1,0:T(8,128)} %bitcast.14, f32[128,128]{1,0:T(8,128)} %bitcast.15, s32[2,128]{1,0:T(2,128)} %bitcast.19, s32[8,128]{1,0:T(8,128)} %bitcast.16, ...), custom_call_target="tpu_custom_call" | custom-call | tf_op jit(solution)/shard_map/parareal/pallas_call | solution.py:575
  88.1 1.5 %copy.13 = f32[1,4,32,128]{3,2,1,0:T(8,128)} copy(f32[1,4,32,128]{3,2,1,0:T(8,128)} %bitcast.10) | data formatting | bytes 131072

commit v5 on v4

--- a/solution.py
+++ b/solution.py
@@ -43,11 +43,16 @@
     block = lax.broadcasted_iota(jnp.int32, shape, len(shape) - 3)
     sub = lax.broadcasted_iota(jnp.int32, shape, len(shape) - 2)
     lane = lax.broadcasted_iota(jnp.int32, shape, len(shape) - 1)
-    row_half = jnp.where((block == 3) & (sub == 7), 0.0, 0.5)
-    col_half = jnp.where(lane == 127, 0.0, 0.5)
-    face_r = row_half * (conductivity + next_rows(conductivity))
-    face_c = col_half * (conductivity + next_cols(conductivity))
-    return face_r, prev_rows(face_r), face_c, prev_cols(face_c)
+    down_half = jnp.where((block == 3) & (sub == 7), 0.0, 0.5)
+    up_half = jnp.where((block == 0) & (sub == 0), 0.0, 0.5)
+    right_half = jnp.where(lane == 127, 0.0, 0.5)
+    left_half = jnp.where(lane == 0, 0.0, 0.5)
+    return (
+        down_half * (conductivity + next_rows(conductivity)),
+        up_half * (conductivity + prev_rows(conductivity)),
+        right_half * (conductivity + next_cols(conductivity)),
+        left_half * (conductivity + prev_cols(conductivity)),
+    )
 
 
 def sweep(v, base, weights):
@@ -213,32 +218,30 @@
     cell_row = (cell >> 7) & 31
     code = (cell >> 12) * 32 + (cell_row & 3) * 8 + (cell_row >> 2)
     cell_lane = cell & 127
-    number = lax.broadcasted_iota(jnp.int32, (128, 128), 0)
+    number = lax.broadcasted_iota(jnp.int32, (64, 128), 0)
+    column_number = lax.broadcasted_iota(jnp.int32, (256, 128), 0)
     for t in range(8):
-        rows_t = jnp.broadcast_to(code[t : t + 1, :], (128, 128))
-        row_hot[t] = jnp.where(rows_t == number, 1.0, 0.0).astype(jnp.bfloat16)
-        lanes_t = jnp.broadcast_to(cell_lane[t : t + 1, :], (128, 128))
-        hot = jnp.where(lanes_t == number, 1.0, 0.0)
+        rows_t = jnp.broadcast_to(code[t : t + 1, :] & 63, (64, 128))
+        row_hot[:, t * 128 : (t + 1) * 128] = jnp.where(rows_t == number, 1.0, 0.0).astype(
+            jnp.bfloat16
+        )
+        columns_t = (code[t : t + 1, :] >> 6) * 128 + cell_lane[t : t + 1, :]
+        hot = jnp.where(jnp.broadcast_to(columns_t, (256, 128)) == column_number, 1.0, 0.0)
         lane_hot[t * 128 : (t + 1) * 128, :] = hot.T.astype(jnp.bfloat16)
 
     def scatter(parts):
-        total = jnp.zeros((128 * len(parts), 128), jnp.float32)
-        for p in range(4):
-            stacked = []
-            for part in parts:
-                pieces = []
-                for t in (2 * p, 2 * p + 1):
-                    line = jnp.broadcast_to(part[t : t + 1, :], (16, 128)).astype(jnp.bfloat16)
-                    block = row_hot[t].reshape(8, 16, 128) * line[None]
-                    pieces.append(block.reshape(128, 128))
-                stacked.append(jnp.concatenate(pieces, axis=1))
-            left = jnp.concatenate(stacked, axis=0)
-            right = lane_hot[p * 256 : (p + 1) * 256, :]
-            total = total + jnp.dot(left, right, preferred_element_type=jnp.float32)
-        result = total[:128]
+        rows = []
+        for part in parts:
+            line = jnp.concatenate([part[t : t + 1, :] for t in range(8)], axis=1)
+            line = jnp.broadcast_to(line, (16, 1024)).astype(jnp.bfloat16)
+            rows.append((row_hot[...].reshape(4, 16, 1024) * line[None]).reshape(64, 1024))
+        left = jnp.concatenate(rows, axis=0)
+        total = jnp.dot(left, lane_hot[...], preferred_element_type=jnp.float32)
+        result = total[:64]
         for n in range(1, len(parts)):
-            result = result + total[n * 128 : (n + 1) * 128]
-        return result.reshape(GROUP, 4, 8, 128)
+            result = result + total[n * 64 : (n + 1) * 64]
+        halves = [result[:, h * 128 : (h + 1) * 128].reshape(GROUP // 2, 4, 8, 128) for h in (0, 1)]
+        return jnp.concatenate(halves, axis=0)
 
     def terms(value, number_of):
         parts = []
@@ -607,8 +610,8 @@
             pltpu.VMEM((shares, peers, 2, 128), f32),
             pltpu.VMEM((peers, 2, 128), f32),
             pltpu.VMEM(whole, f32),
-            pltpu.VMEM((8, 128, 128), jnp.bfloat16),
-            pltpu.VMEM((1024, 128), jnp.bfloat16),
+            pltpu.VMEM((64, 1024), jnp.bfloat16),
+            pltpu.VMEM((1024, 256), jnp.bfloat16),
             pltpu.VMEM((2, 8, 128), jnp.int32),
             pltpu.VMEM((2, 8, 128), jnp.int32),
             pltpu.VMEM((8, 128), jnp.int32),

time: 89.8 us -> 87.1 us (0.970)
  Pallas kernels: 87.5 us -> 84.8 us
    pallas_call x1, Pallas kernels: 87.5 us -> 84.8 us  [body(): pl.pallas_call(functools.partial(kernel, planes, peers), out_shape=jax.Sh...]
where the time goes in v5:
time: 87.1 us; the launch traced here: 86.9 us
  Pallas kernels  84.8 us (97%)
  local copies, waits for them, and re-layouts  1.47 us (2%)
    pallas_call x1, Pallas kernels, body(): pl.pallas_call(functools.partial(kernel, planes, peers), out_shape=jax.Sh...  84.8 us

profile of v5, /device:TPU:448, one launch (start us, length us, event | category | flops | bytes accessed | tf_op | source)
XLA Modules:
  0.0 86.9 jit_solution(12176678449227931531)
XLA Ops:
  0.7 84.8 %parareal.1 = f32[128,128]{1,0:T(8,128)} custom-call(s32[1]{0:T(128)S(6)} %copy.12.count_ref, f32[128,128]{1,0:T(8,128)} %bitcast.11, f32[128,128]{1,0:T(8,128)} %bitcast.12, f32[128,128]{1,0:T(8,128)} %bitcast.13, f32[128,128]{1,0:T(8,128)} %bitcast.14, f32[128,128]{1,0:T(8,128)} %bitcast.15, s32[2,128]{1,0:T(2,128)} %bitcast.19, s32[8,128]{1,0:T(8,128)} %bitcast.16, ...), custom_call_target="tpu_custom_call" | custom-call | tf_op jit(solution)/shard_map/parareal/pallas_call | solution.py:578
  85.4 1.5 %copy.13 = f32[1,4,32,128]{3,2,1,0:T(8,128)} copy(f32[1,4,32,128]{3,2,1,0:T(8,128)} %bitcast.10) | data formatting | bytes 131072

commit v6 on v5

--- a/solution.py
+++ b/solution.py
@@ -37,44 +37,93 @@
     return pltpu.roll(v, 1, v.ndim - 1)
 
 
-def faces(pressure, perm):
+def iota(shape, axis):
+    return lax.broadcasted_iota(jnp.int32, shape, len(shape) + axis)
+
+
+def row_halves(shape):
+    block, sub = iota(shape, -3), iota(shape, -2)
+    return (
+        jnp.where((block == 3) & (sub == 7), 0.0, 0.5),
+        jnp.where((block == 0) & (sub == 0), 0.0, 0.5),
+    )
+
+
+def packed_next(v):
+    return jnp.concatenate([v[:, 1:], pltpu.roll(v[:, :1], 127, v.ndim - 1)], axis=1)
+
+
+def packed_prev(v):
+    return jnp.concatenate([pltpu.roll(v[:, 1:], 1, v.ndim - 1), v[:, :1]], axis=1)
+
+
+def packed_faces(pressure, perm):
     conductivity = perm * jnp.exp(stress_factor * pressure)
     shape = pressure.shape
-    block = lax.broadcasted_iota(jnp.int32, shape, len(shape) - 3)
-    sub = lax.broadcasted_iota(jnp.int32, shape, len(shape) - 2)
-    lane = lax.broadcasted_iota(jnp.int32, shape, len(shape) - 1)
-    down_half = jnp.where((block == 3) & (sub == 7), 0.0, 0.5)
-    up_half = jnp.where((block == 0) & (sub == 0), 0.0, 0.5)
-    right_half = jnp.where(lane == 127, 0.0, 0.5)
-    left_half = jnp.where(lane == 0, 0.0, 0.5)
+    parity, place = iota(shape, -4), iota(shape, -1) & 63
+    down, up = row_halves(shape)
+    right = jnp.where((parity == 1) & (place == 63), 0.0, 0.5)
+    left = jnp.where((parity == 0) & (place == 0), 0.0, 0.5)
     return (
-        down_half * (conductivity + next_rows(conductivity)),
-        up_half * (conductivity + prev_rows(conductivity)),
-        right_half * (conductivity + next_cols(conductivity)),
-        left_half * (conductivity + prev_cols(conductivity)),
-    )
-
-
-def sweep(v, base, weights):
+        down * (conductivity + next_rows(conductivity)),
+        up * (conductivity + prev_rows(conductivity)),
+        right * (conductivity + packed_next(conductivity)),
+        left * (conductivity + packed_prev(conductivity)),
+    )
+
+
+def packed_sweep(v, base, weights):
     down, up, right, left = weights
     return base + (down * next_rows(v) + up * prev_rows(v)) + (
-        right * next_cols(v) + left * prev_cols(v)
+        right * packed_next(v) + left * packed_prev(v)
     )
 
 
 def coarse(pressure, source, store, perm, leak):
-    parts = faces(pressure, perm)
-    inverse = 1.0 / (store + leak + (parts[0] + parts[1]) + (parts[2] + parts[3]))
+    conductivity = perm * jnp.exp(stress_factor * pressure)
+    shape = pressure.shape
+    lane = iota(shape, -1)
+    down_half, up_half = row_halves(shape)
+    down = down_half * (conductivity + next_rows(conductivity))
+    up = up_half * (conductivity + prev_rows(conductivity))
+    right = jnp.where(lane == 127, 0.0, 0.5) * (conductivity + next_cols(conductivity))
+    left = jnp.where(lane == 0, 0.0, 0.5) * (conductivity + prev_cols(conductivity))
+    inverse = 1.0 / (store + leak + (down + up) + (right + left))
     base = (store * pressure + source) * inverse
-    weights = [part * inverse for part in parts]
+    down, up, right, left = down * inverse, up * inverse, right * inverse, left * inverse
     v = pressure
     for _ in range(COARSE_SWEEPS):
-        v = sweep(v, base, weights)
+        v = base + (down * next_rows(v) + up * prev_rows(v)) + (
+            right * next_cols(v) + left * prev_cols(v)
+        )
     return v
 
 
 def pick(table, lanes):
     return jnp.take_along_axis(table, lanes, axis=1, mode="promise_in_bounds")
+
+
+def pack(blocks):
+    lane = lax.broadcasted_iota(jnp.int32, (8, 128), 1)
+    places = 2 * (lane & 63)
+    pairs = []
+    for p in range(GROUP // 2):
+        for e in range(2):
+            for r in range(4):
+                low, high = pick(blocks[2 * p, r], places + e), pick(blocks[2 * p + 1, r], places + e)
+                pairs.append(jnp.where(lane < 64, low, high))
+    return jnp.stack(pairs).reshape(GROUP // 2, 2, 4, 8, 128)
+
+
+def unpack(packed):
+    lane = lax.broadcasted_iota(jnp.int32, (8, 128), 1)
+    places = lane >> 1
+    blocks = []
+    for f in range(GROUP):
+        for r in range(4):
+            even, odd = [pick(packed[f // 2, e, r], places + 64 * (f % 2)) for e in range(2)]
+            blocks.append(jnp.where((lane & 1) == 0, even, odd))
+    return jnp.stack(blocks).reshape(GROUP, 4, 8, 128)
 
 
 def kernel(
@@ -104,7 +153,10 @@
     store,
     perm,
     leak,
-    tisum,
+    fine_store,
+    fine_perm,
+    fine_leak,
+    fine_source,
     own_source,
     source_in,
     u_out,
@@ -123,6 +175,8 @@
     lane_hot,
     export_lane,
     export_code,
+    fine_lane,
+    fine_code,
     trace_lane,
     trace_row,
     weight,
@@ -209,6 +263,9 @@
         row = (cell >> 7) & 31
         export_lane[g] = cell & 127
         export_code[g] = jnp.where((row >> 2) == sub8, (cell >> 12) * 4 + (row & 3), -1)
+        fine_lane[g] = ((cell >> 12) & 1) * 64 + ((cell & 127) >> 1)
+        number = (cell >> 13) * 8 + (cell & 1) * 4 + (row & 3)
+        fine_code[g] = jnp.where((row >> 2) == sub8, number, -1)
     slot = trace_ref[...]
     trace_lane[...] = slot & 127
     trace_row[...] = slot >> 7
@@ -216,17 +273,17 @@
     weight[...] = jnp.where(live, trans_ref[...], 0.0)
     cell = local_ref[...]
     cell_row = (cell >> 7) & 31
-    code = (cell >> 12) * 32 + (cell_row & 3) * 8 + (cell_row >> 2)
-    cell_lane = cell & 127
+    code = (cell & 1) * 32 + (cell_row & 3) * 8 + (cell_row >> 2)
+    cell_column = (cell >> 13) * 128 + ((cell >> 12) & 1) * 64 + ((cell & 127) >> 1)
     number = lax.broadcasted_iota(jnp.int32, (64, 128), 0)
     column_number = lax.broadcasted_iota(jnp.int32, (256, 128), 0)
     for t in range(8):
-        rows_t = jnp.broadcast_to(code[t : t + 1, :] & 63, (64, 128))
+        rows_t = jnp.broadcast_to(code[t : t + 1, :], (64, 128))
         row_hot[:, t * 128 : (t + 1) * 128] = jnp.where(rows_t == number, 1.0, 0.0).astype(
             jnp.bfloat16
         )
-        columns_t = (code[t : t + 1, :] >> 6) * 128 + cell_lane[t : t + 1, :]
-        hot = jnp.where(jnp.broadcast_to(columns_t, (256, 128)) == column_number, 1.0, 0.0)
+        columns_t = jnp.broadcast_to(cell_column[t : t + 1, :], (256, 128))
+        hot = jnp.where(columns_t == column_number, 1.0, 0.0)
         lane_hot[t * 128 : (t + 1) * 128, :] = hot.T.astype(jnp.bfloat16)
 
     def scatter(parts):
@@ -240,7 +297,7 @@
         result = total[:64]
         for n in range(1, len(parts)):
             result = result + total[n * 64 : (n + 1) * 64]
-        halves = [result[:, h * 128 : (h + 1) * 128].reshape(GROUP // 2, 4, 8, 128) for h in (0, 1)]
+        halves = [result[:, h * 128 : (h + 1) * 128].reshape(1, 2, 4, 8, 128) for h in (0, 1)]
         return jnp.concatenate(halves, axis=0)
 
     def terms(value, number_of):
@@ -251,7 +308,11 @@
             value = value - part
         return parts
 
-    tisum[...] = scatter(terms(weight[...], 3))
+    rate = pack(store[...]) * (1.0 / fine_size)
+    fine_store[...] = rate
+    fine_perm[...] = pack(perm[...])
+    fine_leak[...] = rate + pack(leak[...]) + scatter(terms(weight[...], 3))
+    fine_source[...] = pack(own_source[...])
 
     pl.semaphore_wait(barrier, peers - 1 + 2 * (GROUP - 1) + 4)
 
@@ -374,18 +435,19 @@
         source_copy(0, (column + d) % GROUP).start()
     source_in[GROUP + column] = own_source[column]
 
-    def exports(blocks, offset, g):
-        lanes, codes = export_lane[g], export_code[g] - offset
+    def exports(tables, lanes, codes):
         found = jnp.zeros((8, 128), jnp.float32)
-        for n in range(4 * blocks.shape[0]):
-            found = jnp.where(codes == n, pick(blocks[n // 4, n % 4], lanes), found)
+        for n, table in enumerate(tables):
+            found = jnp.where(codes == n, pick(table, lanes), found)
         return jnp.sum(found, axis=0, keepdims=True)
 
     def announce(k):
         for j in range(GROUP):
-            u = u_out[k, j][None]
+            u = u_out[k, j]
             for g in range(2):
-                first_out[k, j, g : g + 1, :] = exports(u, 4 * column, g)
+                first_out[k, j, g : g + 1, :] = exports(
+                    [u[r] for r in range(4)], export_lane[g], export_code[g] - 4 * column
+                )
 
         for d in others:
             for j in range(GROUP):
@@ -456,7 +518,7 @@
             u_arrival(k, (column + d) % GROUP).wait_recv()
 
     def fine(k):
-        field[...] = u_in[k]
+        field[...] = pack(u_in[k])
 
         def step(t, carry):
             m = k * (FINE_STEPS - 1) + t - 1
@@ -465,15 +527,15 @@
             @pl.when(t > 0)
             def _():
                 for g in range(2):
-                    shared[m, me, g : g + 1, :] = exports(q, 0, g)
+                    tables = [q[n // 8, (n // 4) % 2, n % 4] for n in range(16)]
+                    shared[m, me, g : g + 1, :] = exports(tables, fine_lane[g], fine_code[g])
                 for d in others:
                     share_copy(m, (me + d) % peers).start()
 
-            parts = faces(q, perm[...])
-            rate = store[...] * (1.0 / fine_size)
-            total = rate + leak[...] + tisum[...] + (parts[0] + parts[1]) + (parts[2] + parts[3])
+            parts = packed_faces(q, fine_perm[...])
+            total = fine_leak[...] + (parts[0] + parts[1]) + (parts[2] + parts[3])
             inverse = 1.0 / total
-            base = (rate * q + own_source[...]) * inverse
+            base = (fine_store[...] * q + fine_source[...]) * inverse
             weights = [part * inverse for part in parts]
 
             @pl.when(t > 0)
@@ -498,12 +560,12 @@
             base = base + scatter(terms(weight[...] * value, 2)) * inverse
             v = q
             for _ in range(SWEEPS):
-                v = sweep(v, base, weights)
+                v = packed_sweep(v, base, weights)
             field[...] = v
             return carry
 
         lax.fori_loop(0, FINE_STEPS, step, 0)
-        f_out[k] = field[...]
+        f_out[k] = unpack(field[...])
 
         @pl.when(odd == 0)
         def _():
@@ -573,6 +635,7 @@
     f32 = jnp.float32
     block = (4, 8, 128)
     whole = (GROUP,) + block
+    packed = (GROUP // 2, 2) + block
     shares = ITERS * (FINE_STEPS - 1)
     slots = 2 * GROUP
     out = pl.pallas_call(
@@ -595,7 +658,10 @@
             pltpu.VMEM(whole, f32),
             pltpu.VMEM(whole, f32),
             pltpu.VMEM(whole, f32),
-            pltpu.VMEM(whole, f32),
+            pltpu.VMEM(packed, f32),
+            pltpu.VMEM(packed, f32),
+            pltpu.VMEM(packed, f32),
+            pltpu.VMEM(packed, f32),
             pltpu.VMEM(whole, f32),
             pltpu.VMEM((slots,) + block, f32),
             pltpu.VMEM((ITERS + 1,) + whole, f32),
@@ -609,9 +675,11 @@
             pltpu.VMEM((ITERS, GROUP * peers, 2, 128), f32),
             pltpu.VMEM((shares, peers, 2, 128), f32),
             pltpu.VMEM((peers, 2, 128), f32),
-            pltpu.VMEM(whole, f32),
+            pltpu.VMEM(packed, f32),
             pltpu.VMEM((64, 1024), jnp.bfloat16),
             pltpu.VMEM((1024, 256), jnp.bfloat16),
+            pltpu.VMEM((2, 8, 128), jnp.int32),
+            pltpu.VMEM((2, 8, 128), jnp.int32),
             pltpu.VMEM((2, 8, 128), jnp.int32),
             pltpu.VMEM((2, 8, 128), jnp.int32),
             pltpu.VMEM((8, 128), jnp.int32),

time: 87.1 us -> 87.3 us (level)
  no operation moved by 1% of the time
where the time goes in v6:
time: 87.3 us; the launch traced here: 87.1 us
  Pallas kernels  85 us (97%)
  local copies, waits for them, and re-layouts  1.47 us (2%)
    pallas_call x1, Pallas kernels, body(): pl.pallas_call(functools.partial(kernel, planes, peers), out_shape=jax.Sh...  85 us

profile of v6, /device:TPU:448, one launch (start us, length us, event | category | flops | bytes accessed | tf_op | source)
XLA Modules:
  0.0 87.1 jit_solution(2203851741467577338)
XLA Ops:
  0.7 85.0 %parareal.1 = f32[128,128]{1,0:T(8,128)} custom-call(s32[1]{0:T(128)S(6)} %copy.12.count_ref, f32[128,128]{1,0:T(8,128)} %bitcast.11, f32[128,128]{1,0:T(8,128)} %bitcast.12, f32[128,128]{1,0:T(8,128)} %bitcast.13, f32[128,128]{1,0:T(8,128)} %bitcast.14, f32[128,128]{1,0:T(8,128)} %bitcast.15, s32[2,128]{1,0:T(2,128)} %bitcast.19, s32[8,128]{1,0:T(8,128)} %bitcast.16, ...), custom_call_target="tpu_custom_call" | custom-call | tf_op jit(solution)/shard_map/parareal/pallas_call | solution.py:641
  85.7 1.5 %copy.13 = f32[1,4,32,128]{3,2,1,0:T(8,128)} copy(f32[1,4,32,128]{3,2,1,0:T(8,128)} %bitcast.10) | data formatting | bytes 131072

commit v7 on v6

--- a/solution.py
+++ b/solution.py
@@ -199,7 +199,7 @@
     plane = slice_index // GROUP
     column = slice_index % GROUP
     odd = plane % 2
-    partner = plane + 1 - 2 * odd
+    handed = odd * ((plane < planes - 1).astype(jnp.int32) + (plane < planes - 2).astype(jnp.int32))
     others = sorted(range(1, peers), key=lambda d: -min(d, peers - d))
 
     barrier = pltpu.get_barrier_semaphore()
@@ -214,17 +214,17 @@
             device_id={"tm": plane * GROUP + (column + d) % GROUP, "frac": me},
         )
 
-    for d in (1, 2, planes - 2, planes - 1):
+    @pl.when(odd == 1)
+    def _():
+        for x in range(GROUP):
+            pl.semaphore_signal(
+                barrier, inc=1, device_id={"tm": (plane - 1) * GROUP + x, "frac": me}
+            )
+
+    @pl.when(plane > 1)
+    def _():
         pl.semaphore_signal(
-            barrier,
-            inc=1,
-            device_id={"tm": (plane + d) % planes * GROUP + column, "frac": me},
-        )
-    for d in range(1, GROUP):
-        pl.semaphore_signal(
-            barrier,
-            inc=1,
-            device_id={"tm": partner * GROUP + (column + d) % GROUP, "frac": me},
+            barrier, inc=1, device_id={"tm": slice_index - (1 + odd) * GROUP, "frac": me}
         )
 
     pairs = (
@@ -244,7 +244,133 @@
     ]
     for fetch in fetches:
         fetch.start()
-    for fetch in fetches:
+    fetches[0].wait()
+    for f in range(GROUP):
+        for r in range(4):
+            own_source[f, r] = source_ref[pl.ds(f * 32 + r, 8, stride=4), :]
+
+    pl.semaphore_wait(barrier, peers - 1 + GROUP - 1 + (1 - odd) * GROUP + handed)
+
+    def source_copy(ahead, target):
+        slot = (1 - ahead) * GROUP + column
+        return pltpu.make_async_remote_copy(
+            src_ref=own_source.at[target],
+            dst_ref=source_in.at[slot],
+            send_sem=source_send.at[ahead, target],
+            recv_sem=source_recv.at[slot],
+            device_id={"tm": (plane + ahead) * GROUP + target, "frac": me},
+        )
+
+    def source_arrival(slot):
+        return pltpu.make_async_remote_copy(
+            src_ref=own_source.at[0],
+            dst_ref=source_in.at[slot],
+            send_sem=source_send.at[0, 0],
+            recv_sem=source_recv.at[slot],
+            device_id={"tm": plane * GROUP + (column + 1) % GROUP, "frac": me},
+        )
+
+    def u_copy(k, target):
+        return pltpu.make_async_remote_copy(
+            src_ref=u_out.at[k, target],
+            dst_ref=u_in.at[k, column],
+            send_sem=u_send.at[k, target],
+            recv_sem=u_recv.at[k, column],
+            device_id={"tm": plane * GROUP + target, "frac": me},
+        )
+
+    def u_arrival(k, origin):
+        return pltpu.make_async_remote_copy(
+            src_ref=u_out.at[k, origin],
+            dst_ref=u_in.at[k, origin],
+            send_sem=u_send.at[k, origin],
+            recv_sem=u_recv.at[k, origin],
+            device_id={"tm": plane * GROUP + origin, "frac": me},
+        )
+
+    def f_copy(k, ahead, target):
+        slot = (1 - ahead) * GROUP + column
+        return pltpu.make_async_remote_copy(
+            src_ref=f_out.at[k, target],
+            dst_ref=f_in.at[k, slot],
+            send_sem=f_send.at[k, ahead, target],
+            recv_sem=f_recv.at[k, slot],
+            device_id={"tm": (plane + ahead) * GROUP + target, "frac": me},
+        )
+
+    def f_arrival(k, slot):
+        return pltpu.make_async_remote_copy(
+            src_ref=f_out.at[k, 0],
+            dst_ref=f_in.at[k, slot],
+            send_sem=f_send.at[k, 0, 0],
+            recv_sem=f_recv.at[k, slot],
+            device_id={"tm": plane * GROUP + (column + 1) % GROUP, "frac": me},
+        )
+
+    def edge_copy(k, ahead):
+        return pltpu.make_async_remote_copy(
+            src_ref=edge_out.at[k],
+            dst_ref=edge_in.at[k],
+            send_sem=edge_send.at[k, ahead - 1],
+            recv_sem=edge_recv.at[k],
+            device_id={"tm": slice_index + ahead * GROUP, "frac": me},
+        )
+
+    def edge_arrival(k):
+        return pltpu.make_async_remote_copy(
+            src_ref=edge_out.at[k],
+            dst_ref=edge_in.at[k],
+            send_sem=edge_send.at[k, 0],
+            recv_sem=edge_recv.at[k],
+            device_id={"tm": slice_index - GROUP, "frac": me},
+        )
+
+    def first_copy(k, target, peer):
+        return pltpu.make_async_remote_copy(
+            src_ref=first_out.at[k, target],
+            dst_ref=first_in.at[k, column * peers + me],
+            send_sem=first_send.at[k],
+            recv_sem=first_recv.at[k],
+            device_id={"tm": plane * GROUP + target, "frac": peer},
+        )
+
+    def first_all(k):
+        return pltpu.make_async_remote_copy(
+            src_ref=first_in.at[k, pl.ds(0, GROUP * peers - 1)],
+            dst_ref=first_in.at[k, pl.ds(0, GROUP * peers - 1)],
+            send_sem=first_send.at[k],
+            recv_sem=first_recv.at[k],
+            device_id={"tm": slice_index, "frac": (me + 1) % peers},
+        )
+
+    def share_copy(m, target):
+        return pltpu.make_async_remote_copy(
+            src_ref=shared.at[m, me],
+            dst_ref=shared.at[m, me],
+            send_sem=share_send.at[m],
+            recv_sem=share_recv.at[m],
+            device_id={"tm": slice_index, "frac": target},
+        )
+
+    def share_all(m):
+        return pltpu.make_async_remote_copy(
+            src_ref=shared.at[m, pl.ds(0, peers - 1)],
+            dst_ref=shared.at[m, pl.ds(0, peers - 1)],
+            send_sem=share_send.at[m],
+            recv_sem=share_recv.at[m],
+            device_id={"tm": slice_index, "frac": (me + 1) % peers},
+        )
+
+    @pl.when(odd == 0)
+    def _():
+        for d in (2, 1, 3, 0):
+            source_copy(1, (column + d) % GROUP).start()
+
+    for d in (2, 1, 3):
+        source_copy(0, (column + d) % GROUP).start()
+    source_in[GROUP + column] = own_source[column]
+
+    for fetch in fetches[1:]:
         fetch.wait()
 
     for f in range(GROUP):
@@ -254,7 +380,6 @@
             store[f, r] = storage_ref[rows, :]
             perm[f, r] = perm_ref[rows, :]
             leak[f, r] = leak_ref[rows, :]
-            own_source[f, r] = source_ref[rows, :]
 
     sub8 = lax.broadcasted_iota(jnp.int32, (8, 128), 0)
     lane8 = lax.broadcasted_iota(jnp.int32, (8, 128), 1)
@@ -314,126 +439,6 @@
     fine_leak[...] = rate + pack(leak[...]) + scatter(terms(weight[...], 3))
     fine_source[...] = pack(own_source[...])
 
-    pl.semaphore_wait(barrier, peers - 1 + 2 * (GROUP - 1) + 4)
-
-    def source_copy(ahead, target):
-        slot = (1 - ahead) * GROUP + column
-        return pltpu.make_async_remote_copy(
-            src_ref=own_source.at[target],
-            dst_ref=source_in.at[slot],
-            send_sem=source_send.at[ahead, target],
-            recv_sem=source_recv.at[slot],
-            device_id={"tm": (plane + ahead) * GROUP + target, "frac": me},
-        )
-
-    def source_arrival(slot):
-        return pltpu.make_async_remote_copy(
-            src_ref=own_source.at[0],
-            dst_ref=source_in.at[slot],
-            send_sem=source_send.at[0, 0],
-            recv_sem=source_recv.at[slot],
-            device_id={"tm": plane * GROUP + (column + 1) % GROUP, "frac": me},
-        )
-
-    def u_copy(k, target):
-        return pltpu.make_async_remote_copy(
-            src_ref=u_out.at[k, target],
-            dst_ref=u_in.at[k, column],
-            send_sem=u_send.at[k, target],
-            recv_sem=u_recv.at[k, column],
-            device_id={"tm": plane * GROUP + target, "frac": me},
-        )
-
-    def u_arrival(k, origin):
-        return pltpu.make_async_remote_copy(
-            src_ref=u_out.at[k, origin],
-            dst_ref=u_in.at[k, origin],
-            send_sem=u_send.at[k, origin],
-            recv_sem=u_recv.at[k, origin],
-            device_id={"tm": plane * GROUP + origin, "frac": me},
-        )
-
-    def f_copy(k, ahead, target):
-        slot = (1 - ahead) * GROUP + column
-        return pltpu.make_async_remote_copy(
-            src_ref=f_out.at[k, target],
-            dst_ref=f_in.at[k, slot],
-            send_sem=f_send.at[k, ahead, target],
-            recv_sem=f_recv.at[k, slot],
-            device_id={"tm": (plane + ahead) * GROUP + target, "frac": me},
-        )
-
-    def f_arrival(k, slot):
-        return pltpu.make_async_remote_copy(
-            src_ref=f_out.at[k, 0],
-            dst_ref=f_in.at[k, slot],
-            send_sem=f_send.at[k, 0, 0],
-            recv_sem=f_recv.at[k, slot],
-            device_id={"tm": plane * GROUP + (column + 1) % GROUP, "frac": me},
-        )
-
-    def edge_copy(k, ahead):
-        return pltpu.make_async_remote_copy(
-            src_ref=edge_out.at[k],
-            dst_ref=edge_in.at[k],
-            send_sem=edge_send.at[k, ahead - 1],
-            recv_sem=edge_recv.at[k],
-            device_id={"tm": slice_index + ahead * GROUP, "frac": me},
-        )
-
-    def edge_arrival(k):
-        return pltpu.make_async_remote_copy(
-            src_ref=edge_out.at[k],
-            dst_ref=edge_in.at[k],
-            send_sem=edge_send.at[k, 0],
-            recv_sem=edge_recv.at[k],
-            device_id={"tm": slice_index - GROUP, "frac": me},
-        )
-
-    def first_copy(k, target, peer):
-        return pltpu.make_async_remote_copy(
-            src_ref=first_out.at[k, target],
-            dst_ref=first_in.at[k, column * peers + me],
-            send_sem=first_send.at[k],
-            recv_sem=first_recv.at[k],
-            device_id={"tm": plane * GROUP + target, "frac": peer},
-        )
-
-    def first_all(k):
-        return pltpu.make_async_remote_copy(
-            src_ref=first_in.at[k, pl.ds(0, GROUP * peers - 1)],
-            dst_ref=first_in.at[k, pl.ds(0, GROUP * peers - 1)],
-            send_sem=first_send.at[k],
-            recv_sem=first_recv.at[k],
-            device_id={"tm": slice_index, "frac": (me + 1) % peers},
-        )
-
-    def share_copy(m, target):
-        return pltpu.make_async_remote_copy(
-            src_ref=shared.at[m, me],
-            dst_ref=shared.at[m, me],
-            send_sem=share_send.at[m],
-            recv_sem=share_recv.at[m],
-            device_id={"tm": slice_index, "frac": target},
-        )
-
-    def share_all(m):
-        return pltpu.make_async_remote_copy(
-            src_ref=shared.at[m, pl.ds(0, peers - 1)],
-            dst_ref=shared.at[m, pl.ds(0, peers - 1)],
-            send_sem=share_send.at[m],
-            recv_sem=share_recv.at[m],
-            device_id={"tm": slice_index, "frac": (me + 1) % peers},
-        )
-
-    @pl.when(odd == 0)
-    def _():
-        for d in (2, 1, 3, 0):
-            source_copy(1, (column + d) % GROUP).start()
-
-    for d in (2, 1, 3):
-        source_copy(0, (column + d) % GROUP).start()
-    source_in[GROUP + column] = own_source[column]
 
     def exports(tables, lanes, codes):
         found = jnp.zeros((8, 128), jnp.float32)

time: 87.3 us -> 83.4 us (0.955)
  Pallas kernels: 85 us -> 81 us
    pallas_call x1, Pallas kernels: 85 us -> 81 us  [body(): pl.pallas_call(functools.partial(kernel, planes, peers), out_shape=jax.Sh...]
where the time goes in v7:
time: 83.4 us; the launch traced here: 83.1 us
  Pallas kernels  81 us (97%)
  local copies, waits for them, and re-layouts  1.47 us (2%)
    pallas_call x1, Pallas kernels, body(): pl.pallas_call(functools.partial(kernel, planes, peers), out_shape=jax.Sh...  81 us

profile of v7, /device:TPU:448, one launch (start us, length us, event | category | flops | bytes accessed | tf_op | source)
XLA Modules:
  0.0 83.1 jit_solution(9737366699618011066)
XLA Ops:
  0.7 81.0 %parareal.1 = f32[128,128]{1,0:T(8,128)} custom-call(s32[1]{0:T(128)S(6)} %copy.12.count_ref, f32[128,128]{1,0:T(8,128)} %bitcast.11, f32[128,128]{1,0:T(8,128)} %bitcast.12, f32[128,128]{1,0:T(8,128)} %bitcast.13, f32[128,128]{1,0:T(8,128)} %bitcast.14, f32[128,128]{1,0:T(8,128)} %bitcast.15, s32[2,128]{1,0:T(2,128)} %bitcast.19, s32[8,128]{1,0:T(8,128)} %bitcast.16, ...), custom_call_target="tpu_custom_call" | custom-call | tf_op jit(solution)/shard_map/parareal/pallas_call | solution.py:646
  81.7 1.5 %copy.13 = f32[1,4,32,128]{3,2,1,0:T(8,128)} copy(f32[1,4,32,128]{3,2,1,0:T(8,128)} %bitcast.10) | data formatting | bytes 131072

commit v8 on v7

--- a/solution.py
+++ b/solution.py
@@ -542,6 +542,7 @@
             inverse = 1.0 / total
             base = (fine_store[...] * q + fine_source[...]) * inverse
             weights = [part * inverse for part in parts]
+            first_sweep = packed_sweep(q, base, weights)
 
             @pl.when(t > 0)
             def _():
@@ -562,9 +563,10 @@
             for n in range(2 * peers):
                 line = jnp.broadcast_to(gathered[n // 2, n % 2 : n % 2 + 1, :], (8, 128))
                 value = jnp.where(rows == n, pick(line, lanes), value)
-            base = base + scatter(terms(weight[...] * value, 2)) * inverse
-            v = q
-            for _ in range(SWEEPS):
+            coupled = scatter(terms(weight[...] * value, 2)) * inverse
+            base = base + coupled
+            v = first_sweep + coupled
+            for _ in range(SWEEPS - 1):
                 v = packed_sweep(v, base, weights)
             field[...] = v
             return carry

time: 83.4 us -> 83.3 us (level)
  no operation moved by 1% of the time
where the time goes in v8:
time: 83.3 us; the launch traced here: 83.1 us
  Pallas kernels  81 us (97%)
  local copies, waits for them, and re-layouts  1.47 us (2%)
    pallas_call x1, Pallas kernels, body(): pl.pallas_call(functools.partial(kernel, planes, peers), out_shape=jax.Sh...  81 us

profile of v8, /device:TPU:448, one launch (start us, length us, event | category | flops | bytes accessed | tf_op | source)
XLA Modules:
  0.0 83.1 jit_solution(13834970589490541246)
XLA Ops:
  0.7 81.0 %parareal.1 = f32[128,128]{1,0:T(8,128)} custom-call(s32[1]{0:T(128)S(6)} %copy.12.count_ref, f32[128,128]{1,0:T(8,128)} %bitcast.11, f32[128,128]{1,0:T(8,128)} %bitcast.12, f32[128,128]{1,0:T(8,128)} %bitcast.13, f32[128,128]{1,0:T(8,128)} %bitcast.14, f32[128,128]{1,0:T(8,128)} %bitcast.15, s32[2,128]{1,0:T(2,128)} %bitcast.19, s32[8,128]{1,0:T(8,128)} %bitcast.16, ...), custom_call_target="tpu_custom_call" | custom-call | tf_op jit(solution)/shard_map/parareal/pallas_call | solution.py:648
  81.6 1.5 %copy.13 = f32[1,4,32,128]{3,2,1,0:T(8,128)} copy(f32[1,4,32,128]{3,2,1,0:T(8,128)} %bitcast.10) | data formatting | bytes 131072

commit v9 on v7

--- a/solution.py
+++ b/solution.py
@@ -129,7 +129,7 @@
 def kernel(
     planes,
     peers,
-    count_ref,
+    count_hbm,
     pressure_hbm,
     storage_hbm,
     perm_hbm,
@@ -140,6 +140,7 @@
     trace_hbm,
     trans_hbm,
     out_ref,
+    count_ref,
     pressure_ref,
     storage_ref,
     perm_ref,
@@ -202,31 +203,6 @@
     handed = odd * ((plane < planes - 1).astype(jnp.int32) + (plane < planes - 2).astype(jnp.int32))
     others = sorted(range(1, peers), key=lambda d: -min(d, peers - d))
 
-    barrier = pltpu.get_barrier_semaphore()
-    for d in others:
-        pl.semaphore_signal(
-            barrier, inc=1, device_id={"tm": slice_index, "frac": (me + d) % peers}
-        )
-    for d in range(1, GROUP):
-        pl.semaphore_signal(
-            barrier,
-            inc=1,
-            device_id={"tm": plane * GROUP + (column + d) % GROUP, "frac": me},
-        )
-
-    @pl.when(odd == 1)
-    def _():
-        for x in range(GROUP):
-            pl.semaphore_signal(
-                barrier, inc=1, device_id={"tm": (plane - 1) * GROUP + x, "frac": me}
-            )
-
-    @pl.when(plane > 1)
-    def _():
-        pl.semaphore_signal(
-            barrier, inc=1, device_id={"tm": slice_index - (1 + odd) * GROUP, "frac": me}
-        )
-
     pairs = (
         (source_hbm, source_ref),
         (pressure_hbm, pressure_ref),
@@ -237,6 +213,7 @@
         (local_hbm, local_ref),
         (trace_hbm, trace_ref),
         (trans_hbm, trans_ref),
+        (count_hbm, count_ref),
     )
     fetches = [
         pltpu.make_async_copy(origin, target, fetched.at[n])
@@ -244,6 +221,32 @@
     ]
     for fetch in fetches:
         fetch.start()
+
+    barrier = pltpu.get_barrier_semaphore()
+    for d in others:
+        pl.semaphore_signal(
+            barrier, inc=1, device_id={"tm": slice_index, "frac": (me + d) % peers}
+        )
+    for d in range(1, GROUP):
+        pl.semaphore_signal(
+            barrier,
+            inc=1,
+            device_id={"tm": plane * GROUP + (column + d) % GROUP, "frac": me},
+        )
+
+    @pl.when(odd == 1)
+    def _():
+        for x in range(GROUP):
+            pl.semaphore_signal(
+                barrier, inc=1, device_id={"tm": (plane - 1) * GROUP + x, "frac": me}
+            )
+
+    @pl.when(plane > 1)
+    def _():
+        pl.semaphore_signal(
+            barrier, inc=1, device_id={"tm": slice_index - (1 + odd) * GROUP, "frac": me}
+        )
+
     fetches[0].wait()
     for f in range(GROUP):
         for r in range(4):
@@ -646,10 +649,10 @@
     out = pl.pallas_call(
         functools.partial(kernel, planes, peers),
         out_shape=jax.ShapeDtypeStruct((128, 128), f32),
-        in_specs=[pl.BlockSpec(memory_space=pltpu.SMEM)]
-        + [pl.BlockSpec(memory_space=pl.ANY)] * 9,
+        in_specs=[pl.BlockSpec(memory_space=pl.ANY)] * 10,
         out_specs=vmem,
         scratch_shapes=[
+            pltpu.SMEM((1,), jnp.int32),
             pltpu.VMEM((128, 128), f32),
             pltpu.VMEM((128, 128), f32),
             pltpu.VMEM((128, 128), f32),
@@ -690,7 +693,7 @@
             pltpu.VMEM((8, 128), jnp.int32),
             pltpu.VMEM((8, 128), jnp.int32),
             pltpu.VMEM((8, 128), f32),
-            pltpu.SemaphoreType.DMA((9,)),
+            pltpu.SemaphoreType.DMA((10,)),
             pltpu.SemaphoreType.DMA((2, GROUP)),
             pltpu.SemaphoreType.DMA((slots,)),
             pltpu.SemaphoreType.DMA((ITERS + 1, GROUP)),

time: 83.4 us -> 83.4 us (level)
  no operation moved by 1% of the time
where the time goes in v9:
time: 83.4 us; the launch traced here: 83.2 us
  Pallas kernels  81 us (97%)
  local copies, waits for them, and re-layouts  1.47 us (2%)
    pallas_call x1, Pallas kernels, body(): pl.pallas_call(functools.partial(kernel, planes, peers), out_shape=jax.Sh...  81 us

profile of v9, /device:TPU:448, one launch (start us, length us, event | category | flops | bytes accessed | tf_op | source)
XLA Modules:
  0.0 83.2 jit_solution(12886115729358020195)
XLA Ops:
  0.7 81.0 %parareal.1 = f32[128,128]{1,0:T(8,128)} custom-call(s32[1]{0:T(128)S(6)} %copy.12.count_hbm, f32[128,128]{1,0:T(8,128)} %bitcast.11, f32[128,128]{1,0:T(8,128)} %bitcast.12, f32[128,128]{1,0:T(8,128)} %bitcast.13, f32[128,128]{1,0:T(8,128)} %bitcast.14, f32[128,128]{1,0:T(8,128)} %bitcast.15, s32[2,128]{1,0:T(2,128)} %bitcast.19, s32[8,128]{1,0:T(8,128)} %bitcast.16, ...), custom_call_target="tpu_custom_call" | custom-call | tf_op jit(solution)/shard_map/parareal/pallas_call | solution.py:649
  81.7 1.5 %copy.13 = f32[1,4,32,128]{3,2,1,0:T(8,128)} copy(f32[1,4,32,128]{3,2,1,0:T(8,128)} %bitcast.10) | data formatting | bytes 131072
